TPU v7x, 256 devices: a whole 4x4x8 slice. The times are simulated.
256 devices in a mesh: gx: 32 (over x, z), gy: 8 (over y, core).
Axes of the slice: x: 4, y: 4, z: 8, core: 2. Of those that a mesh axis runs over, the one named last changes fastest.
Arguments:
- flow_state: float32 [4, 512, 256, 128], P(None, 'gx', 'gy'), may hold values from -10 to 10
- viscosity: float32 [512, 256, 128], P('gx', 'gy'), may hold values from 300 to 1200
Outputs:
- flow_next: float32 [4, 512, 256, 128], P(None, 'gx', 'gy')
All inputs are finite; a program needn't handle non-finite values.
Results may differ from a plain program's by a relative error of at most 0.0003.
Values sent between devices are 32-bit elements; how exact they have to be, the bound alone decides.
A program may use at most 64 MiB of HBM per device.

v0:
```python
import jax
import jax.numpy as jnp
from jax import lax
from jax.sharding import Mesh
from jax.sharding import PartitionSpec as P

GX = ("gx_0", "gx_1")


ADVECT = 0.2
BUOYANT = 0.5
CONDUCT = 0.6


def in_blocks(array, dim, peers):
    dims = array.shape
    blocks = array.reshape(*dims[:dim], peers, dims[dim] // peers, *dims[dim + 1 :])
    return jnp.moveaxis(blocks, dim, 0)


def laid_out(blocks, dim):
    blocks = jnp.moveaxis(blocks, 0, dim)
    dims = blocks.shape
    return blocks.reshape(*dims[:dim], dims[dim] * dims[dim + 1], *dims[dim + 2 :])


def exchange_in_order(blocks, axes, turns):
    inside = blocks.shape[1:]
    result = blocks.reshape(*(lax.axis_size(a) for a in axes), *inside)
    for k in turns:
        result = lax.all_to_all(result, axes[k], k, k, tiled=True)
    return result.reshape(-1, *inside)


def exchange_by_axis(array, axes, turns, split_dim, concat_dim):
    blocks = in_blocks(array, split_dim, lax.axis_size(axes))
    return laid_out(exchange_in_order(blocks, axes, turns), concat_dim)


def padded_2(array, sides, width):
    edges = {}
    for axis, dim in sides:
        peers, length = (lax.axis_size(axis), array.shape[dim])
        up = [(i, (i + 1) % peers) for i in range(peers - 1)]
        last = lax.slice_in_dim(array, length - width, length, axis=dim)
        first = lax.slice_in_dim(array, 0, width, axis=dim)
        edges[dim] = (
            lax.ppermute(last, axis, up),
            lax.ppermute(first, axis, [(b, a) for a, b in up]),
        )
    done = []
    for _, dim in sides:
        low, high = edges[dim]
        around = [(width, width) if d in done else (0, 0) for d in range(array.ndim)]
        array = jnp.concatenate([jnp.pad(low, around), array, jnp.pad(high, around)], axis=dim)
        done.append(dim)
    return array


def in_one_piece(arrays, axis, split_dim, concat_dim, along):
    widths = [a.shape[along] for a in arrays]
    both = jnp.concatenate(arrays, axis=along)
    result = lax.all_to_all(both, axis, split_axis=split_dim, concat_axis=concat_dim, tiled=True)
    return tuple(jnp.split(result, [sum(widths[:k]) for k in range(1, len(widths))], axis=along))


def slice_at(array, position, along):
    return lax.index_in_dim(array, position, along, keepdims=False)


def advect(flow_state, padded):
    along_x = 0.5 * (padded[:, 2:, 1:-1] - padded[:, :-2, 1:-1])
    along_y = 0.5 * (padded[:, 1:-1, 2:] - padded[:, 1:-1, :-2])
    along_z = 0.5 * (jnp.roll(flow_state, -1, 3) - jnp.roll(flow_state, 1, 3))
    carried = flow_state[0:1] * along_x + flow_state[1:2] * along_y + flow_state[2:3] * along_z
    source = flow_state - ADVECT * carried
    return jnp.concatenate([source[:2], source[2:3] + BUOYANT * flow_state[3:4], source[3:]], 0)


def edge_faces(viscosity, neighbours, along, at_start, at_end):
    length = viscosity.shape[along]
    before = jnp.where(
        at_start,
        lax.slice_in_dim(viscosity, 0, 1, axis=along),
        lax.slice_in_dim(neighbours, 0, 1, axis=along),
    )
    beyond = jnp.where(
        at_end,
        lax.slice_in_dim(viscosity, length - 1, length, axis=along),
        lax.slice_in_dim(neighbours, length + 1, length + 2, axis=along),
    )
    extended = jnp.concatenate([before, viscosity, beyond], along)
    face_values = 0.5 * (
        lax.slice_in_dim(extended, 0, length + 1, axis=along)
        + lax.slice_in_dim(extended, 1, length + 2, axis=along)
    )
    scales = jnp.array([1.0, 1.0, 1.0, CONDUCT], jnp.float32).reshape(4, 1, 1, 1)
    return scales * face_values[None]


def factor(lowers, middle, uppers):
    inverse, ratios = ([], [])
    for k in range(len(middle)):
        divisor = middle[k] if k == 0 else middle[k] - lowers[k] * ratios[k - 1]
        inverse.append(1.0 / divisor)
        ratios.append(uppers[k] * inverse[k])
    return (inverse, ratios)


def sweep_down(values, lowers, inverse, ratios):
    forward = []
    for k in range(len(values)):
        running = values[k] if k == 0 else values[k] - lowers[k] * forward[k - 1]
        forward.append(running * inverse[k])
    result = [forward[-1]]
    for k in range(len(values) - 2, -1, -1):
        result.append(forward[k] - ratios[k] * result[-1])
    return result[::-1]


def pack_rows(row_pair):
    stacked = jnp.stack(row_pair, 0)
    return jnp.transpose(stacked, (0, 2, 1, 3)).reshape(2, -1, stacked.shape[-1])


def spread_groups(piece):
    split = piece.reshape(piece.shape[0], piece.shape[1] // 2, 2, piece.shape[2])
    velocity = split[:, :, 0:1]
    spread = jnp.concatenate([velocity, velocity, velocity, split[:, :, 1:2]], 2)
    return spread.reshape(piece.shape[0], -1, piece.shape[2])


def prepare(faces, along):
    length = faces.shape[along] - 1
    face_list = [slice_at(faces, i, along) for i in range(length + 1)]
    lowers = [-face_list[i] for i in range(length)]
    uppers = [-face_list[i + 1] for i in range(length)]
    middle = [1.0 + face_list[i] + face_list[i + 1] for i in range(length)]
    inverse, ratios = factor(lowers[1:-1], middle[1:-1], uppers[1:-1])
    empty_row = jnp.zeros_like(middle[0])
    interior_rows = length - 2
    first_column = sweep_down(
        [-lowers[1]] + [empty_row] * (interior_rows - 1), lowers[1:-1], inverse, ratios
    )
    last_column = sweep_down(
        [empty_row] * (interior_rows - 1) + [-uppers[length - 2]], lowers[1:-1], inverse, ratios
    )
    below = (lowers[0], lowers[-1] * first_column[-1])
    centre = (middle[0] + uppers[0] * first_column[0], middle[-1] + lowers[-1] * last_column[-1])
    above = (uppers[0] * last_column[0], uppers[-1])
    return {
        "lowers": lowers,
        "uppers": uppers,
        "inverse": inverse,
        "ratios": ratios,
        "first_column": first_column,
        "last_column": last_column,
        "field_rows": (pack_rows(below), pack_rows(centre), pack_rows(above)),
        "group_rows": (
            pack_rows((below[0][0::3], below[1][0::3])),
            pack_rows((centre[0][0::3], centre[1][0::3])),
            pack_rows((above[0][0::3], above[1][0::3])),
        ),
    }


def reduced_solve(below, centre, above, source):
    length = centre.shape[0]
    position = lax.broadcasted_iota(jnp.int32, centre.shape, 0)
    below = jnp.where(position == 0, 0.0, below)
    above = jnp.where(position == length - 1, 0.0, above)
    solution = lax.linalg.tridiagonal_solve(
        jnp.moveaxis(below, 0, -1),
        jnp.moveaxis(centre, 0, -1),
        jnp.moveaxis(above, 0, -1),
        jnp.moveaxis(source, 0, -1)[..., None],
    )[..., 0]
    return jnp.moveaxis(solution, -1, 0)


def right_sides(field, factors, along):
    length = field.shape[along]
    values = [slice_at(field, i, along) for i in range(length)]
    interior = sweep_down(
        values[1:-1], factors["lowers"][1:-1], factors["inverse"], factors["ratios"]
    )
    first = values[0] - factors["uppers"][0] * interior[0]
    last = values[-1] - factors["lowers"][-1] * interior[-1]
    return (pack_rows((first, last)), interior)


def assemble(returned, interior, factors, along):
    unpacked = returned.reshape(2, returned.shape[1] // 4, 4, returned.shape[2])
    unpacked = jnp.transpose(unpacked, (0, 2, 1, 3))
    start, finish = (unpacked[0], unpacked[1])
    middle_rows = [
        interior[k] + factors["first_column"][k] * start + factors["last_column"][k] * finish
        for k in range(len(interior))
    ]
    return jnp.stack([start] + middle_rows + [finish], along)


def solve_along_x(field, factors, kept_rows):
    packed, interior = right_sides(field, factors, 1)
    received = lax.all_to_all(packed, GX, split_axis=1, concat_axis=0, tiled=True)
    solution = reduced_solve(kept_rows[0], kept_rows[1], kept_rows[2], received)
    returned = exchange_by_axis(solution, GX, (0, 1), 0, 1)
    return assemble(returned, interior, factors, 1)


def solve_along_y(field, factors, kept_rows):
    packed, interior = right_sides(field, factors, 2)
    received = lax.all_to_all(packed, "gy", split_axis=1, concat_axis=0, tiled=True)
    solution = reduced_solve(kept_rows[0], kept_rows[1], kept_rows[2], received)
    returned = lax.all_to_all(solution, "gy", split_axis=0, concat_axis=1, tiled=True)
    return assemble(returned, interior, factors, 2)


def per_device(flow_state, viscosity):
    neighbours = padded_2(viscosity, ((GX, 0), ("gy", 1)), 1)
    x_index = lax.axis_index(GX)
    y_index = lax.axis_index("gy")
    faces_x = edge_faces(
        viscosity, neighbours[:, 1:-1], 0, x_index == 0, x_index == lax.axis_size(GX) - 1
    )
    faces_y = edge_faces(
        viscosity, neighbours[1:-1], 1, y_index == 0, y_index == lax.axis_size("gy") - 1
    )
    factors_x = prepare(faces_x, 1)
    factors_y = prepare(faces_y, 2)
    kept_x = None
    kept_y = None
    group_x = factors_x["group_rows"]
    received_x = in_one_piece((group_x[0], group_x[1], group_x[2]), GX, 1, 0, 2)
    kept_x = tuple((spread_groups(piece) for piece in received_x))
    group_y = factors_y["group_rows"]
    received_y = in_one_piece((group_y[0], group_y[1], group_y[2]), "gy", 1, 0, 2)
    kept_y = tuple((spread_groups(piece) for piece in received_y))
    current = flow_state
    padded = padded_2(current, ((GX, 1), ("gy", 2)), 1)
    source = advect(current, padded)
    current = solve_along_y(solve_along_x(source, factors_x, kept_x), factors_y, kept_y)
    return current


def solution(mesh):
    torus = Mesh(mesh.devices.reshape(4, 8, mesh.shape["gy"]), ("gx_0", "gx_1", "gy"))
    placed = (P(None, GX, "gy", None), P(GX, "gy", None))
    return jax.shard_map(
        per_device, mesh=torus, in_specs=placed, out_specs=P(None, GX, "gy", None), check_vma=False
    )
```

profile of v0, /device:TPU:1, one launch (start us, length us, event | category | flops | bytes accessed | tf_op | source)
XLA Modules:
  0.0 163.2 jit_solution(2691300131745059006)
XLA Ops:
  0.0 0.8 fusion.837
  0.8 4.3 %collective-permute-start.4 = (f32[1,32,128]{2,1,0:T(8,128)S(1)}, f32[1,32,128]{2,1,0:T(8,128)S(1)}, u32[]{:S(2)}, u32[]{:S(2)}) collective-permute-start(f32[1,32,128]{2,1,0:T(8,128)S(1)} %get-tuple-element.561), channel_id=1, source_target_pairs={{0,8},{8,16},{16,24},{24,32},{32,40},{40,48},{48,56},{56,64},{64,7... | collective-permute-start | bytes 49160 | tf_op jit(solution)/shard_map/ppermute | solution.py:48
  5.2 1.3 collective-permute-start.5
  6.5 1.5 fusion.836
  8.0 4.8 %collective-permute-start.1 = (f32[4,1,32,128]{3,2,1,0:T(8,128)}, f32[4,1,32,128]{3,2,1,0:T(8,128)}, u32[]{:S(2)}, u32[]{:S(2)}) collective-permute-start(f32[4,1,32,128]{3,2,1,0:T(8,128)} %get-tuple-element.557), channel_id=1, source_target_pairs={{0,8},{8,16},{16,24},{24,32},{32,40},{40,48},{48,56},{56,64},{64,7... | collective-permute-start | bytes 196616 | tf_op jit(solution)/shard_map/ppermute | solution.py:48
  12.8 0.9 fusion.838
  13.7 4.4 %collective-permute-start.6 = (f32[16,1,128]{2,1,0:T(1,128)S(1)}, f32[16,1,128]{2,1,0:T(1,128)S(1)}, u32[]{:S(2)}, u32[]{:S(2)}) collective-permute-start(f32[16,1,128]{2,1,0:T(1,128)S(1)} %get-tuple-element.565), channel_id=1, source_target_pairs={{0,1},{1,2},{2,3},{3,4},{4,5},{5,6},{6,7},{8,9},{9,10},{10,11},{11... | collective-permute-start | bytes 24584 | tf_op jit(solution)/shard_map/ppermute | solution.py:48
  18.1 1.9 %collective-permute-start.7 = (f32[16,1,128]{2,1,0:T(1,128)S(1)}, f32[16,1,128]{2,1,0:T(1,128)S(1)}, u32[]{:S(2)}, u32[]{:S(2)}) collective-permute-start(f32[16,1,128]{2,1,0:T(1,128)S(1)} %get-tuple-element.564), channel_id=1, source_target_pairs={{1,0},{2,1},{3,2},{4,3},{5,4},{6,5},{7,6},{9,8},{10,9},{11,10},{12... | collective-permute-start | bytes 24584 | tf_op jit(solution)/shard_map/ppermute | solution.py:49
  20.0 2.0 %multiply_bitcast_fusion.2 = (f32[16,32,128]{2,1,0:T(8,128)S(1)}, f32[16,32,128]{2,1,0:T(8,128)}, f32[16,32,128]{2,1,0:T(8,128)}) fusion(f32[4,16,32,128]{3,2,1,0:T(8,128)} %param.4), kind=kLoop, calls=%fused_computation.186 | loop fusion | flops 196608 | bytes 1572864 | tf_op jit(solution)/shard_map/mul | solution.py:75
  22.0 1.7 %fusion.833 = (f32[4,16,32,1]{3,2,1,0:T(8,128)}, f32[4,16,32,1]{3,2,1,0:T(8,128)}) fusion(f32[4,16,32,128]{3,2,1,0:T(8,128)S(1)} %copy-done), kind=kLoop, calls=%fused_computation.2052 | loop fusion | bytes 32768 | tf_op jit(solution)/shard_map/jit(_roll_static)/slice | solution.py:74
  23.7 1.7 %fusion.834 = (f32[4,16,32,127]{3,2,1,0:T(8,128)}, f32[4,16,32,127]{3,2,1,0:T(8,128)}) fusion(f32[4,16,32,128]{3,2,1,0:T(8,128)S(1)} %copy-done), kind=kLoop, calls=%fused_computation.2053 | loop fusion | bytes 4161536 | tf_op jit(solution)/shard_map/jit(_roll_static)/slice | solution.py:74
  27.8 1.3 collective-permute-start
  29.1 1.9 %collective-permute-start.2 = (f32[4,16,1,128]{3,2,1,0:T(1,128)}, f32[4,16,1,128]{3,2,1,0:T(1,128)S(1)}, u32[]{:S(2)}, u32[]{:S(2)}) collective-permute-start(f32[4,16,1,128]{3,2,1,0:T(1,128)} %get-tuple-element.554), channel_id=1, source_target_pairs={{1,0},{2,1},{3,2},{4,3},{5,4},{6,5},{7,6},{9,8},{10,9},{11,10},{12... | collective-permute-start | bytes 98312 | tf_op jit(solution)/shard_map/ppermute | solution.py:49
  31.5 0.8 fusion.302
  32.9 0.9 fusion.132
  33.8 0.8 subtract_multiply_fusion.139
  35.6 5.1 %all-to-all-start.5 = ((f32[2,32,384]{2,0,1:T(2,128)}), f32[2,32,384]{2,0,1:T(2,128)}, u32[]{:S(2)}, u32[]{:S(2)}) async-start(f32[2,32,384]{2,0,1:T(2,128)} %copy.2038), calls=%async_computation.5 | async-start | bytes 196608 | tf_op jit(solution)/shard_map/all_to_all | solution.py:63
  40.8 3.5 %collective-permute-start.3 = (f32[4,16,1,128]{3,2,1,0:T(1,128)}, f32[4,16,1,128]{3,2,1,0:T(1,128)S(1)}, u32[]{:S(2)}, u32[]{:S(2)}) collective-permute-start(f32[4,16,1,128]{3,2,1,0:T(1,128)} %get-tuple-element.555), channel_id=1, source_target_pairs={{0,1},{1,2},{2,3},{3,4},{4,5},{5,6},{6,7},{8,9},{9,10},{10,11},{11... | collective-permute-start | bytes 98312 | tf_op jit(solution)/shard_map/ppermute | solution.py:48
  46.0 1.1 constant_dynamic-update-slice_fusion.2
  47.1 1.0 constant_dynamic-update-slice_fusion
  48.7 1.9 %fusion.5 = f32[4,16,32,128]{3,2,1,0:T(8,128)S(1)} fusion(f32[4,16,32,128]{3,2,1,0:T(8,128)S(1)} %copy-done, f32[4,18,32,128]{3,2,1,0:T(8,128)S(1)} %constant_dynamic-update-slice_fusion, f32[4,16,1,128]{3,2,1,0:T(1,128)S(1)} %collective-permute-done.3, f32[4,16,1,128]{3,2,1,0:T(1,128)S(1)} %collective-permute-done.2, ...), kind=kLoop, calls=%fused_computation.6 | loop fusion | flops 5767168 | bytes 6356992 | tf_op jit(solution)/shard_map/sub | solution.py:76
  50.8 1.4 fusion.39
  53.1 0.8 copy.1903
  55.3 13.6 %all-to-all-start = ((f32[2,128,128]{2,0,1:T(2,128)}), f32[2,128,128]{2,0,1:T(2,128)S(1)}, u32[]{:S(2)}, u32[]{:S(2)}) async-start(f32[2,128,128]{2,0,1:T(2,128)} %copy.1895), calls=%async_computation | async-start | bytes 262144 | tf_op jit(solution)/shard_map/all_to_all | solution.py:205
  68.9 0.9 copy.2039
  70.7 1.4 select_bitcast_fusion
  72.1 6.7 %all-to-all-done = f32[2,128,128]{2,0,1:T(2,128)S(1)} async-done(((f32[2,128,128]{2,0,1:T(2,128)}), f32[2,128,128]{2,0,1:T(2,128)S(1)}, u32[]{:S(2)}, u32[]{:S(2)}) %all-to-all-start) | async-done | bytes 131104 | tf_op jit(solution)/shard_map/all_to_all | solution.py:205
  79.5 4.1 %all-to-all-start.1 = ((f32[2,64,384]{2,0,1:T(2,128)}), f32[2,64,384]{2,0,1:T(2,128)S(1)}, u32[]{:S(2)}, u32[]{:S(2)}) async-start(f32[2,64,384]{2,0,1:T(2,128)} %copy.1903), calls=%async_computation.1 | async-start | bytes 393216 | tf_op jit(solution)/shard_map/all_to_all | solution.py:63
  83.5 0.9 copy.1896
  87.8 4.9 %all-to-all-done.1 = f32[2,64,384]{2,0,1:T(2,128)S(1)} async-done(((f32[2,64,384]{2,0,1:T(2,128)}), f32[2,64,384]{2,0,1:T(2,128)S(1)}, u32[]{:S(2)}, u32[]{:S(2)}) %all-to-all-start.1) | async-done | bytes 196640 | tf_op jit(solution)/shard_map/all_to_all | solution.py:63
  95.7 1.5 bitcast_divide_fusion.15
  99.3 3.9 %all-to-all-start.2 = ((f32[4,8,2,4,128]{4,2,1,3,0:T(2,128)}), f32[4,8,2,4,128]{4,2,1,3,0:T(2,128)}, u32[]{:S(2)}, u32[]{:S(2)}) async-start(f32[4,8,2,4,128]{4,2,1,3,0:T(2,128)} %copy.1968), calls=%async_computation.2 | async-start | bytes 262144 | tf_op jit(solution)/shard_map/all_to_all | solution.py:31
  103.9 4.2 %all-to-all-done.2 = f32[4,8,2,4,128]{4,2,1,3,0:T(2,128)} async-done(((f32[4,8,2,4,128]{4,2,1,3,0:T(2,128)}), f32[4,8,2,4,128]{4,2,1,3,0:T(2,128)}, u32[]{:S(2)}, u32[]{:S(2)}) %all-to-all-start.2) | async-done | bytes 131104 | tf_op jit(solution)/shard_map/all_to_all | solution.py:31
  108.1 1.6 copy.1969
  109.7 4.2 %all-to-all-start.3 = ((f32[4,8,2,4,128]{4,2,0,3,1:T(2,128)}), f32[4,8,2,4,128]{4,2,0,3,1:T(2,128)}, u32[]{:S(2)}, u32[]{:S(2)}) async-start(f32[4,8,2,4,128]{4,2,0,3,1:T(2,128)} %copy.1969), calls=%async_computation.3 | async-start | bytes 262144 | tf_op jit(solution)/shard_map/all_to_all | solution.py:31
  113.9 1.5 slice_bitcast_fusion.12
  115.4 6.6 %all-to-all-done.3 = f32[4,8,2,4,128]{4,2,0,3,1:T(2,128)} async-done(((f32[4,8,2,4,128]{4,2,0,3,1:T(2,128)}), f32[4,8,2,4,128]{4,2,0,3,1:T(2,128)}, u32[]{:S(2)}, u32[]{:S(2)}) %all-to-all-start.3) | async-done | bytes 131104 | tf_op jit(solution)/shard_map/all_to_all | solution.py:31
  121.9 1.0 copy.2212
  123.0 2.4 %constant_dynamic-update-slice_fusion.80 = (f32[4,16,32,128]{3,2,0,1:T(8,128)S(1)}, f32[4,1,32,128]{3,2,0,1:T(8,128)S(1)}, f32[4,1,32,128]{3,2,0,1:T(8,128)S(1)}...) fusion(f32[4,16,32,128]{3,2,0,1:T(8,128)S(1)} %constant_dynamic, ...), kind=kLoop, calls=%fused_computation.134 | loop fusion | flops 3047424 | bytes 5898240
  127.7 1.8 %subtract_multiply_fusion.112 = (f32[4,16,1,128]{3,0,1,2:T(4,128)}, f32[4,16,1,128]{3,0,1,2:T(4,128)S(1)}, f32[4,16,1,128]{3,0,1,2:T(4,128)}, f32[4,16,1,128]{3,...) fusion(f32[4,16,1,128]{3,0,1,2:T(4,128)S(1)} %bitcast.9260, ...), kind=kLoop, calls=%fused_computation.1064 | loop fusion | flops 2244608 | bytes 4489216 | tf_op jit(solution)/shard_map/mul | solution.py:114
  129.5 1.0 fusion.300
  131.9 9.4 %all-to-all-start.4 = ((f32[2,64,128]{2,0,1:T(2,128)}), f32[2,64,128]{2,0,1:T(2,128)S(1)}, u32[]{:S(2)}, u32[]{:S(2)}) async-start(f32[2,64,128]{2,0,1:T(2,128)} %copy.2033), calls=%async_computation.4 | async-start | bytes 131072 | tf_op jit(solution)/shard_map/all_to_all | solution.py:213
  141.3 4.8 %all-to-all-done.4 = f32[2,64,128]{2,0,1:T(2,128)S(1)} async-done(((f32[2,64,128]{2,0,1:T(2,128)}), f32[2,64,128]{2,0,1:T(2,128)S(1)}, u32[]{:S(2)}, u32[]{:S(2)}) %all-to-all-start.4) | async-done | bytes 65568 | tf_op jit(solution)/shard_map/all_to_all | solution.py:213
  146.1 0.8 fusion.353
  147.0 0.8 subtract_bitcast_fusion
  148.0 8.0 %all_to_all.97 = f32[16,8,128]{2,1,0:T(8,128)S(1)} all-to-all(f32[16,8,128]{2,1,0:T(8,128)S(1)} %maximum_bitcast_fusion.7), channel_id=1, replica_groups=mesh['gx_0'=4,'gx_1'=8,'gy'=8] {'gy'}, dimensions={0} | all-to-all | bytes 131072 | tf_op jit(solution)/shard_map/all_to_all | solution.py:215
  156.1 3.2 %constant_dynamic-update-slice_fusion.127 = (f32[4,16,32,128]{3,0,1,2:T(4,128)S(1)}, f32[4,16,1,128]{3,0,1,2:T(4,128)S(1)}, f32[4,16,1,128]{3,0,1,2:T(4,128)S(1)...) fusion(f32[4,16,32,128]{3,0,1,2:T(4,128)S(1)} %constant_dynamic, ...), kind=kLoop, calls=%fused_computation.181 | loop fusion | flops 3309568 | bytes 6324224
  161.6 1.6 copy.2098
  (383 shorter events, 24.5 us)
Async XLA Ops:
  0.0 22.0 %copy-start = (f32[4,16,32,128]{3,2,1,0:T(8,128)S(1)}, f32[4,16,32,128]{3,2,1,0:T(8,128)}, u32[]{:S(2)}) copy-start(f32[4,16,32,128]{3,2,1,0:T(8,128)} %param.4) | copy-start | bytes 3145732
  0.8 39.9 %collective-permute-start.4 = (f32[1,32,128]{2,1,0:T(8,128)S(1)}, f32[1,32,128]{2,1,0:T(8,128)S(1)}, u32[]{:S(2)}, u32[]{:S(2)}) collective-permute-start(f32[1,32,128]{2,1,0:T(8,128)S(1)} %get-tuple-element.561), channel_id=1, source_target_pairs={{0,8},{8,16},{16,24},{24,32},{32,40},{40,48},{48,56},{56,64},{64,7... | collective-permute-start | bytes 49160 | tf_op jit(solution)/shard_map/ppermute | solution.py:48
  5.2 39.1 %collective-permute-start.5 = (f32[1,32,128]{2,1,0:T(8,128)S(1)}, f32[1,32,128]{2,1,0:T(8,128)S(1)}, u32[]{:S(2)}, u32[]{:S(2)}) collective-permute-start(f32[1,32,128]{2,1,0:T(8,128)S(1)} %get-tuple-element.560), channel_id=1, source_target_pairs={{8,0},{16,8},{24,16},{32,24},{40,32},{48,40},{56,48},{64,56},{72,6... | collective-permute-start | bytes 49160 | tf_op jit(solution)/shard_map/ppermute | solution.py:49
  8.0 38.0 %collective-permute-start.1 = (f32[4,1,32,128]{3,2,1,0:T(8,128)}, f32[4,1,32,128]{3,2,1,0:T(8,128)}, u32[]{:S(2)}, u32[]{:S(2)}) collective-permute-start(f32[4,1,32,128]{3,2,1,0:T(8,128)} %get-tuple-element.557), channel_id=1, source_target_pairs={{0,8},{8,16},{16,24},{24,32},{32,40},{40,48},{48,56},{56,64},{64,7... | collective-permute-start | bytes 196616 | tf_op jit(solution)/shard_map/ppermute | solution.py:48
  13.7 14.1 %collective-permute-start.6 = (f32[16,1,128]{2,1,0:T(1,128)S(1)}, f32[16,1,128]{2,1,0:T(1,128)S(1)}, u32[]{:S(2)}, u32[]{:S(2)}) collective-permute-start(f32[16,1,128]{2,1,0:T(1,128)S(1)} %get-tuple-element.565), channel_id=1, source_target_pairs={{0,1},{1,2},{2,3},{3,4},{4,5},{5,6},{6,7},{8,9},{9,10},{10,11},{11... | collective-permute-start | bytes 24584 | tf_op jit(solution)/shard_map/ppermute | solution.py:48
  18.1 10.9 %collective-permute-start.7 = (f32[16,1,128]{2,1,0:T(1,128)S(1)}, f32[16,1,128]{2,1,0:T(1,128)S(1)}, u32[]{:S(2)}, u32[]{:S(2)}) collective-permute-start(f32[16,1,128]{2,1,0:T(1,128)S(1)} %get-tuple-element.564), channel_id=1, source_target_pairs={{1,0},{2,1},{3,2},{4,3},{5,4},{6,5},{7,6},{9,8},{10,9},{11,10},{12... | collective-permute-start | bytes 24584 | tf_op jit(solution)/shard_map/ppermute | solution.py:49
  23.7 7.3 %copy-start.5 = (f32[16,32,128]{2,1,0:T(8,128)S(1)}, f32[16,32,128]{2,1,0:T(8,128)}, u32[]{:S(2)}) copy-start(f32[16,32,128]{2,1,0:T(8,128)} %param.5) | copy-start | bytes 786436
  25.4 5.7 %copy-start.76 = (f32[4]{0:T(128)S(1)}, f32[4]{0:T(128)}, u32[]{:S(2)}) copy-start(f32[4]{0:T(128)} %constant.67.clone) | copy-start | bytes 52
  27.8 19.4 %collective-permute-start = (f32[4,1,32,128]{3,2,1,0:T(8,128)}, f32[4,1,32,128]{3,2,1,0:T(8,128)}, u32[]{:S(2)}, u32[]{:S(2)}) collective-permute-start(f32[4,1,32,128]{3,2,1,0:T(8,128)} %get-tuple-element.556), channel_id=1, source_target_pairs={{8,0},{16,8},{24,16},{32,24},{40,32},{48,40},{56,48},{64,56},{72,6... | collective-permute-start | bytes 196616 | tf_op jit(solution)/shard_map/ppermute | solution.py:49
  29.1 19.1 %collective-permute-start.2 = (f32[4,16,1,128]{3,2,1,0:T(1,128)}, f32[4,16,1,128]{3,2,1,0:T(1,128)S(1)}, u32[]{:S(2)}, u32[]{:S(2)}) collective-permute-start(f32[4,16,1,128]{3,2,1,0:T(1,128)} %get-tuple-element.554), channel_id=1, source_target_pairs={{1,0},{2,1},{3,2},{4,3},{5,4},{6,5},{7,6},{9,8},{10,9},{11,10},{12... | collective-permute-start | bytes 98312 | tf_op jit(solution)/shard_map/ppermute | solution.py:49
  35.6 19.7 %all-to-all-start.5 = ((f32[2,32,384]{2,0,1:T(2,128)}), f32[2,32,384]{2,0,1:T(2,128)}, u32[]{:S(2)}, u32[]{:S(2)}) async-start(f32[2,32,384]{2,0,1:T(2,128)} %copy.2038), calls=%async_computation.5 | async-start | bytes 196608 | tf_op jit(solution)/shard_map/all_to_all | solution.py:63
  40.8 7.4 %collective-permute-start.3 = (f32[4,16,1,128]{3,2,1,0:T(1,128)}, f32[4,16,1,128]{3,2,1,0:T(1,128)S(1)}, u32[]{:S(2)}, u32[]{:S(2)}) collective-permute-start(f32[4,16,1,128]{3,2,1,0:T(1,128)} %get-tuple-element.555), channel_id=1, source_target_pairs={{0,1},{1,2},{2,3},{3,4},{4,5},{5,6},{6,7},{8,9},{9,10},{10,11},{11... | collective-permute-start | bytes 98312 | tf_op jit(solution)/shard_map/ppermute | solution.py:48
  45.5 2.6 %copy-start.3 = (f32[4,16,32,127]{3,2,1,0:T(8,128)S(1)}, f32[4,16,32,127]{3,2,1,0:T(8,128)}, u32[]{:S(2)}) copy-start(f32[4,16,32,127]{3,2,1,0:T(8,128)} %get-tuple-element.552) | copy-start | bytes 3121156
  45.6 2.6 %copy-start.4 = (f32[4,16,32,127]{3,2,1,0:T(8,128)S(1)}, f32[4,16,32,127]{3,2,1,0:T(8,128)}, u32[]{:S(2)}) copy-start(f32[4,16,32,127]{3,2,1,0:T(8,128)} %get-tuple-element.553) | copy-start | bytes 3121156
  45.9 2.3 %copy-start.6 = (f32[16,32,128]{2,1,0:T(8,128)S(1)}, f32[16,32,128]{2,1,0:T(8,128)}, u32[]{:S(2)}) copy-start(f32[16,32,128]{2,1,0:T(8,128)} %get-tuple-element.548) | copy-start | bytes 786436
  45.9 2.3 %copy-start.7 = (f32[16,32,128]{2,1,0:T(8,128)S(1)}, f32[16,32,128]{2,1,0:T(8,128)}, u32[]{:S(2)}) copy-start(f32[16,32,128]{2,1,0:T(8,128)} %get-tuple-element.549) | copy-start | bytes 786436
  55.3 23.5 %all-to-all-start = ((f32[2,128,128]{2,0,1:T(2,128)}), f32[2,128,128]{2,0,1:T(2,128)S(1)}, u32[]{:S(2)}, u32[]{:S(2)}) async-start(f32[2,128,128]{2,0,1:T(2,128)} %copy.1895), calls=%async_computation | async-start | bytes 262144 | tf_op jit(solution)/shard_map/all_to_all | solution.py:205
  79.5 13.3 %all-to-all-start.1 = ((f32[2,64,384]{2,0,1:T(2,128)}), f32[2,64,384]{2,0,1:T(2,128)S(1)}, u32[]{:S(2)}, u32[]{:S(2)}) async-start(f32[2,64,384]{2,0,1:T(2,128)} %copy.1903), calls=%async_computation.1 | async-start | bytes 393216 | tf_op jit(solution)/shard_map/all_to_all | solution.py:63
  93.1 2.2 %copy-start.36 = (f32[4,128,1,1]{1,2,0,3:T(1,128)S(1)}, f32[4,128,1,1]{1,2,0,3:T(1,128)}, u32[]{:S(2)}) copy-start(f32[4,128,1,1]{1,2,0,3:T(1,128)} %slice.2540) | copy-start | bytes 6148
  93.1 2.2 %copy-start.39 = (f32[1,4,128,1]{2,0,1,3:T(1,128)S(1)}, f32[1,4,128,1]{2,0,1,3:T(1,128)}, u32[]{:S(2)}) copy-start(f32[1,4,128,1]{2,0,1,3:T(1,128)} %get-tuple-element.607) | copy-start | bytes 6148
  93.1 2.2 %copy-start.40 = (f32[1,4,128,1]{2,0,1,3:T(1,128)S(1)}, f32[1,4,128,1]{2,0,1,3:T(1,128)}, u32[]{:S(2)}) copy-start(f32[1,4,128,1]{2,0,1,3:T(1,128)} %get-tuple-element.608) | copy-start | bytes 6148
  93.1 2.2 %copy-start.41 = (f32[1,4,128,1]{2,0,1,3:T(1,128)S(1)}, f32[1,4,128,1]{2,0,1,3:T(1,128)}, u32[]{:S(2)}) copy-start(f32[1,4,128,1]{2,0,1,3:T(1,128)} %get-tuple-element.609) | copy-start | bytes 6148
  93.1 2.2 %copy-start.42 = (f32[1,4,128,1]{2,0,1,3:T(1,128)S(1)}, f32[1,4,128,1]{2,0,1,3:T(1,128)}, u32[]{:S(2)}) copy-start(f32[1,4,128,1]{2,0,1,3:T(1,128)} %get-tuple-element.610) | copy-start | bytes 6148
  93.1 2.2 %copy-start.43 = (f32[1,4,128,1]{2,0,1,3:T(1,128)S(1)}, f32[1,4,128,1]{2,0,1,3:T(1,128)}, u32[]{:S(2)}) copy-start(f32[1,4,128,1]{2,0,1,3:T(1,128)} %get-tuple-element.611) | copy-start | bytes 6148
  93.1 2.2 %copy-start.44 = (f32[1,4,128,1]{2,0,1,3:T(1,128)S(1)}, f32[1,4,128,1]{2,0,1,3:T(1,128)}, u32[]{:S(2)}) copy-start(f32[1,4,128,1]{2,0,1,3:T(1,128)} %get-tuple-element.612) | copy-start | bytes 6148
  93.1 2.2 %copy-start.45 = (f32[1,4,128,1]{2,0,1,3:T(1,128)S(1)}, f32[1,4,128,1]{2,0,1,3:T(1,128)}, u32[]{:S(2)}) copy-start(f32[1,4,128,1]{2,0,1,3:T(1,128)} %get-tuple-element.613) | copy-start | bytes 6148
  93.1 2.2 %copy-start.46 = (f32[1,4,128,1]{2,0,1,3:T(1,128)S(1)}, f32[1,4,128,1]{2,0,1,3:T(1,128)}, u32[]{:S(2)}) copy-start(f32[1,4,128,1]{2,0,1,3:T(1,128)} %get-tuple-element.614) | copy-start | bytes 6148
  93.1 2.2 %copy-start.47 = (f32[1,4,128,1]{2,0,1,3:T(1,128)S(1)}, f32[1,4,128,1]{2,0,1,3:T(1,128)}, u32[]{:S(2)}) copy-start(f32[1,4,128,1]{2,0,1,3:T(1,128)} %get-tuple-element.615) | copy-start | bytes 6148
  93.2 2.2 %copy-start.48 = (f32[1,4,128,1]{2,0,1,3:T(1,128)S(1)}, f32[1,4,128,1]{2,0,1,3:T(1,128)}, u32[]{:S(2)}) copy-start(f32[1,4,128,1]{2,0,1,3:T(1,128)} %get-tuple-element.616) | copy-start | bytes 6148
  93.2 2.2 %copy-start.49 = (f32[1,4,128,1]{2,0,1,3:T(1,128)S(1)}, f32[1,4,128,1]{2,0,1,3:T(1,128)}, u32[]{:S(2)}) copy-start(f32[1,4,128,1]{2,0,1,3:T(1,128)} %get-tuple-element.617) | copy-start | bytes 6148
  93.7 3.5 %copy-start.37 = (f32[1,4,128,1]{2,0,1,3:T(1,128)S(1)}, f32[1,4,128,1]{2,0,1,3:T(1,128)}, u32[]{:S(2)}) copy-start(f32[1,4,128,1]{2,0,1,3:T(1,128)} %get-tuple-element.588) | copy-start | bytes 6148
  93.7 3.5 %copy-start.38 = (f32[1,4,128,1]{2,0,1,3:T(1,128)S(1)}, f32[1,4,128,1]{2,0,1,3:T(1,128)}, u32[]{:S(2)}) copy-start(f32[1,4,128,1]{2,0,1,3:T(1,128)} %get-tuple-element.569) | copy-start | bytes 6148
  98.3 24.6 %copy-start.8 = (f32[4,1,32,128]{3,2,0,1:T(8,128)S(1)}, f32[4,1,32,128]{3,2,0,1:T(8,128)}, u32[]{:S(2)}) copy-start(f32[4,1,32,128]{3,2,0,1:T(8,128)} %get-tuple-element.278) | copy-start | bytes 196612
  98.3 24.6 %copy-start.9 = (f32[4,1,32,128]{3,2,0,1:T(8,128)S(1)}, f32[4,1,32,128]{3,2,0,1:T(8,128)}, u32[]{:S(2)}) copy-start(f32[4,1,32,128]{3,2,0,1:T(8,128)} %get-tuple-element.289) | copy-start | bytes 196612
  99.3 8.8 %all-to-all-start.2 = ((f32[4,8,2,4,128]{4,2,1,3,0:T(2,128)}), f32[4,8,2,4,128]{4,2,1,3,0:T(2,128)}, u32[]{:S(2)}, u32[]{:S(2)}) async-start(f32[4,8,2,4,128]{4,2,1,3,0:T(2,128)} %copy.1968), calls=%async_computation.2 | async-start | bytes 262144 | tf_op jit(solution)/shard_map/all_to_all | solution.py:31
  109.7 12.2 %all-to-all-start.3 = ((f32[4,8,2,4,128]{4,2,0,3,1:T(2,128)}), f32[4,8,2,4,128]{4,2,0,3,1:T(2,128)}, u32[]{:S(2)}, u32[]{:S(2)}) async-start(f32[4,8,2,4,128]{4,2,0,3,1:T(2,128)} %copy.1969), calls=%async_computation.3 | async-start | bytes 262144 | tf_op jit(solution)/shard_map/all_to_all | solution.py:31
  122.9 2.5 %copy-start.16 = (f32[4,1,32,128]{3,2,0,1:T(8,128)S(1)}, f32[4,1,32,128]{3,2,0,1:T(8,128)}, u32[]{:S(2)}) copy-start(f32[4,1,32,128]{3,2,0,1:T(8,128)} %get-tuple-element.286) | copy-start | bytes 196612
  123.0 2.5 %copy-start.17 = (f32[4,1,32,128]{3,2,0,1:T(8,128)S(1)}, f32[4,1,32,128]{3,2,0,1:T(8,128)}, u32[]{:S(2)}) copy-start(f32[4,1,32,128]{3,2,0,1:T(8,128)} %get-tuple-element.305) | copy-start | bytes 196612
  130.5 10.8 %copy-start.34 = (f32[8,128,16]{1,0,2:T(8,128)S(1)}, f32[8,128,16]{1,0,2:T(8,128)}, u32[]{:S(2)}) copy-start(f32[8,128,16]{1,0,2:T(8,128)} %select_bitcast_fusion) | copy-start | bytes 196612
  130.5 15.7 %copy-start.35 = (f32[15,8,128]{2,1,0:T(8,128)S(1)}, f32[15,8,128]{2,1,0:T(8,128)}, u32[]{:S(2)}) copy-start(f32[15,8,128]{2,1,0:T(8,128)} %get-tuple-element.642) | copy-start | bytes 184324
  131.8 24.2 %copy-start.21 = (f32[4,16,1,128]{3,0,1,2:T(4,128)S(1)}, f32[4,16,1,128]{3,0,1,2:T(4,128)}, u32[]{:S(2)}) copy-start(f32[4,16,1,128]{3,0,1,2:T(4,128)} %get-tuple-element.196) | copy-start | bytes 98308
  131.8 24.2 %copy-start.22 = (f32[4,16,1,128]{3,0,1,2:T(4,128)S(1)}, f32[4,16,1,128]{3,0,1,2:T(4,128)}, u32[]{:S(2)}) copy-start(f32[4,16,1,128]{3,0,1,2:T(4,128)} %get-tuple-element.154) | copy-start | bytes 98308
  131.8 24.2 %copy-start.23 = (f32[4,16,1,128]{3,0,1,2:T(4,128)S(1)}, f32[4,16,1,128]{3,0,1,2:T(4,128)}, u32[]{:S(2)}) copy-start(f32[4,16,1,128]{3,0,1,2:T(4,128)} %get-tuple-element.158) | copy-start | bytes 98308
  131.8 24.2 %copy-start.24 = (f32[4,16,1,128]{3,0,1,2:T(4,128)S(1)}, f32[4,16,1,128]{3,0,1,2:T(4,128)}, u32[]{:S(2)}) copy-start(f32[4,16,1,128]{3,0,1,2:T(4,128)} %get-tuple-element.162) | copy-start | bytes 98308
  131.8 24.2 %copy-start.25 = (f32[4,16,1,128]{3,0,1,2:T(4,128)S(1)}, f32[4,16,1,128]{3,0,1,2:T(4,128)}, u32[]{:S(2)}) copy-start(f32[4,16,1,128]{3,0,1,2:T(4,128)} %get-tuple-element.166) | copy-start | bytes 98308
  131.9 24.2 %copy-start.26 = (f32[4,16,1,128]{3,0,1,2:T(4,128)S(1)}, f32[4,16,1,128]{3,0,1,2:T(4,128)}, u32[]{:S(2)}) copy-start(f32[4,16,1,128]{3,0,1,2:T(4,128)} %get-tuple-element.170) | copy-start | bytes 98308
  131.9 14.2 %all-to-all-start.4 = ((f32[2,64,128]{2,0,1:T(2,128)}), f32[2,64,128]{2,0,1:T(2,128)S(1)}, u32[]{:S(2)}, u32[]{:S(2)}) async-start(f32[2,64,128]{2,0,1:T(2,128)} %copy.2033), calls=%async_computation.4 | async-start | bytes 131072 | tf_op jit(solution)/shard_map/all_to_all | solution.py:213
  156.1 3.4 %copy-start.33 = (f32[4,16,1,128]{3,0,1,2:T(4,128)S(1)}, f32[4,16,1,128]{3,0,1,2:T(4,128)}, u32[]{:S(2)}) copy-start(f32[4,16,1,128]{3,0,1,2:T(4,128)} %get-tuple-element.198) | copy-start | bytes 98308
  (44 other events, 74.8 us)
where the time goes:
time: 165 us; the launch traced here: 163 us
  starting transfers between devices  63.8 us (39%)
  other arithmetic  32.9 us (20%)
  local copies, waits for them, and re-layouts  29.2 us (18%)
  waiting for transfers between devices  27.3 us (17%)
  blocking collectives  8 us (5%)
  between operations  2.04 us (1%)
    ppermute x4, starting transfers between devices, padded_2(): lax.ppermute(last, axis, up)  17.1 us
    all_to_all x1, starting transfers between devices, solve_along_x(): lax.all_to_all(packed, GX, split_axis=1, concat_axis=0, tiled=True)  13.6 us
    all_to_all x2, waiting for transfers between devices, exchange_in_order(): result = lax.all_to_all(result, axes[k], k, k, tiled=True)  10.8 us
    all_to_all x1, starting transfers between devices, solve_along_y(): lax.all_to_all(packed, 'gy', split_axis=1, concat_axis=0, tiled=True)  9.37 us
    all_to_all x2, starting transfers between devices, in_one_piece(): lax.all_to_all(both, axis, split_axis=split_dim, concat_axis=concat_dim,...  9.18 us
    all_to_all x2, starting transfers between devices, exchange_in_order(): result = lax.all_to_all(result, axes[k], k, k, tiled=True)  8.13 us
    all_to_all x1, blocking collectives, solve_along_y(): lax.all_to_all(solution, 'gy', split_axis=0, concat_axis=1, tiled=True)  8 us
    unnamed x82, other arithmetic  7.85 us
  transfers between devices with their start and end apart: 14, of which 5 were waited for; matrix products, arithmetic and copies ran while one was open for 21% of the time, Pallas kernels for 0%

commit v1 on v0

v1 whole, which is shorter than its diff:
```python
import functools

import jax
import jax.numpy as jnp
from jax import lax
from jax.experimental import pallas as pl
from jax.experimental.pallas import tpu as pltpu
from jax.sharding import PartitionSpec as P

MESH = pl.DeviceIdType.MESH

ADVECT = 0.2
BUOYANT = 0.5
CONDUCT = 0.6
KINDS = (1.0, CONDUCT)
KIND_OF = (0, 0, 0, 1)

NF = 4
LX, LY, NZ = 16, 32, 128
PX, PY = 32, 8
Y0 = 8


def factor(faces, along):
    inverse, lower, ratio = {}, {}, {}
    one = jnp.ones_like(faces[1])
    running = one
    forward = {}
    for k in range(1, along - 1):
        centre = 1.0 + faces[k] + faces[k + 1]
        if k > 1:
            centre = centre - faces[k] * ratio[k - 1]
        inverse[k] = 1.0 / centre
        lower[k] = faces[k] * inverse[k]
        ratio[k] = faces[k + 1] * inverse[k]
        running = lower[k] * running
        forward[k] = running
    first, last = {along - 1: jnp.zeros_like(one)}, {along - 1: one}
    for k in range(along - 2, 0, -1):
        first[k] = forward[k] + ratio[k] * first[k + 1]
        last[k] = ratio[k] * last[k + 1]
    first[0], last[0] = one, jnp.zeros_like(one)
    return inverse, lower, ratio, first, last


def keep_factor(load, along, refs, tiles):
    inv_ref, low_ref, rat_ref, first_ref, last_ref = refs
    cells = [load(k) for k in range(along)]
    middles = [None] + [cells[k - 1] + cells[k] for k in range(1, along)]
    tiles[0] = cells[0]
    tiles[1] = cells[-1]
    for kind, scale in enumerate(KINDS):
        faces = [None] + [(0.5 * scale) * m for m in middles[1:]]
        inverse, lower, ratio, first, last = factor(faces, along)
        for k in range(1, along - 1):
            inv_ref[kind, k] = inverse[k]
            low_ref[kind, k] = lower[k]
            rat_ref[kind, k] = ratio[k]
        for k in range(along):
            first_ref[kind, k] = first[k]
            last_ref[kind, k] = last[k]
        tiles[2 + kind] = 1.0 + faces[1] * (1.0 - first[1])
        tiles[4 + kind] = faces[1] * last[1]
        tiles[6 + kind] = 1.0 + faces[along - 1] * (1.0 - last[along - 2])


def rolled(value):
    return pltpu.roll(value, 4, 0)


def interface_factor(coef, base, blocks, refs):
    inv_ref, low_ref, rat_ref = refs
    sub = lax.broadcasted_iota(jnp.int32, (8, NZ), 0)
    down = sub < 4
    thermal = (sub == 3) | (sub == 7)

    def row(block, r):
        return jnp.broadcast_to(coef[pl.ds(base(block) + r, 1), :], (8, NZ))

    def by_kind(block, r):
        return jnp.where(thermal, row(block, r + 1), row(block, r))

    scale = jnp.where(thermal, CONDUCT, 1.0).astype(jnp.float32)
    half = blocks // 2
    sides = []
    for i in range(half + 1):
        if i == 0:
            value = jnp.where(down, row(0, 0), row(blocks - 1, 1))
        elif i == half:
            value = 0.5 * (row(i - 1, 1) + row(i, 0))
        else:
            value = 0.5 * jnp.where(
                down,
                row(i - 1, 1) + row(i, 0),
                row(blocks - 1 - i, 1) + row(blocks - i, 0),
            )
        sides.append(scale * value)
    ratio = None
    for i in range(half):
        j = blocks - 1 - i
        couple = jnp.where(down, by_kind(i, 4), by_kind(j, 4))
        even = jnp.where(down, by_kind(i, 2), by_kind(j, 6)) + sides[i]
        odd = jnp.where(down, by_kind(i, 6), by_kind(j, 2)) + sides[i + 1]
        for m, centre, before, after in (
            (2 * i, even, sides[i], couple),
            (2 * i + 1, odd, couple, sides[i + 1]),
        ):
            if m > 0:
                centre = centre - before * ratio
            inverse = 1.0 / centre
            ratio = after * inverse
            inv_ref[m] = inverse
            low_ref[m] = before * inverse
            rat_ref[m] = ratio
    inv_ref[blocks] = 1.0 / (1.0 - ratio * rolled(ratio))


def interface_solve(right, solved, base, blocks, refs):
    inv_ref, low_ref, rat_ref = refs
    down = lax.broadcasted_iota(jnp.int32, (8, NZ), 0) < 4
    half = blocks // 2
    forward = []
    for i in range(half):
        j = blocks - 1 - i
        mine, other = right[pl.ds(base(i), 8), :], right[pl.ds(base(j), 8), :]
        even = jnp.where(down, mine, other)
        odd = rolled(jnp.where(down, other, mine))
        for m, value in ((2 * i, even), (2 * i + 1, odd)):
            value = inv_ref[m] * value
            if m > 0:
                value = value + low_ref[m] * forward[-1]
            forward.append(value)
    tail = forward[-1]
    values = [None] * blocks
    values[-1] = (tail + rat_ref[blocks - 1] * rolled(tail)) * inv_ref[blocks]
    for m in range(blocks - 2, -1, -1):
        values[m] = forward[m] + rat_ref[m] * values[m + 1]
    for i in range(half):
        j = blocks - 1 - i
        even, odd = values[2 * i], rolled(values[2 * i + 1])
        solved[pl.ds(base(i), 8), :] = jnp.where(down, even, odd)
        solved[pl.ds(base(j), 8), :] = jnp.where(down, odd, even)


def kernel(flow, visc, out, fpad, vbuf, cur, inner, outbuf, *rest):
    xf, yf = rest[0:5], rest[5:10]
    xi, yi = rest[10:13], rest[13:19]
    yi = (yi[0:3], yi[3:6])
    cxs, cxr, cys, cyr, xs, xr, xb, xg, ys, yr, yb, yg = rest[19:31]
    in_sem, out_sem, send_sem, recv_sem, halo_send, halo_recv = rest[31:]
    gx, gy = lax.axis_index("gx"), lax.axis_index("gy")

    barrier = pltpu.get_barrier_semaphore()

    def on_x(d):
        return (lax.rem(gx + d, PX), gy)

    def on_y(d):
        return (gx, lax.rem(gy + d, PY))

    @pl.loop(1, PX)
    def _(d):
        pl.semaphore_signal(barrier, inc=1, device_id=on_x(d), device_id_type=MESH)

    @pl.loop(1, PY)
    def _(d):
        pl.semaphore_signal(barrier, inc=1, device_id=on_y(d), device_id_type=MESH)

    visc_in = pltpu.make_async_copy(visc, vbuf, in_sem.at[0])
    flow_in = pltpu.make_async_copy(
        flow, fpad.at[:, pl.ds(1, LX), pl.ds(Y0, LY), :], in_sem.at[1]
    )
    visc_in.start()
    flow_in.start()

    @pl.when(gx == 0)
    def _():
        fpad[:, 0, Y0 : Y0 + LY, :] = jnp.zeros((NF, LY, NZ), jnp.float32)

    @pl.when(gx == PX - 1)
    def _():
        fpad[:, LX + 1, Y0 : Y0 + LY, :] = jnp.zeros((NF, LY, NZ), jnp.float32)

    @pl.when(gy == 0)
    def _():
        fpad[:, 1 : LX + 1, Y0 - 1 : Y0, :] = jnp.zeros((NF, LX, 1, NZ), jnp.float32)

    @pl.when(gy == PY - 1)
    def _():
        fpad[:, 1 : LX + 1, Y0 + LY : Y0 + LY + 1, :] = jnp.zeros((NF, LX, 1, NZ), jnp.float32)

    visc_in.wait()
    tiles = {}
    keep_factor(lambda k: vbuf[pl.ds(k * LY, LY), :], LX, xf, tiles)
    for r in range(8):
        cxs[pl.ds(r, LY, stride=8), :] = tiles[r]
    tiles = {}
    keep_factor(lambda k: vbuf[pl.ds(k, LX, stride=LY), :], LY, yf, tiles)
    for r in range(8):
        cys[pl.ds(r, LX, stride=8), :] = tiles[r]

    flow_in.wait()
    pl.semaphore_wait(barrier, PX - 1 + PY - 1)

    x_low = fpad.at[:, pl.ds(0, 1), pl.ds(Y0, LY), :]
    x_first = fpad.at[:, pl.ds(1, 1), pl.ds(Y0, LY), :]
    x_last = fpad.at[:, pl.ds(LX, 1), pl.ds(Y0, LY), :]
    x_high = fpad.at[:, pl.ds(LX + 1, 1), pl.ds(Y0, LY), :]
    y_low = fpad.at[:, pl.ds(1, LX), pl.ds(Y0 - 1, 1), :]
    y_first = fpad.at[:, pl.ds(1, LX), pl.ds(Y0, 1), :]
    y_last = fpad.at[:, pl.ds(1, LX), pl.ds(Y0 + LY - 1, 1), :]
    y_high = fpad.at[:, pl.ds(1, LX), pl.ds(Y0 + LY, 1), :]

    def halo(n, src, dst, device):
        return pltpu.make_async_remote_copy(
            src_ref=src,
            dst_ref=dst,
            send_sem=halo_send.at[n],
            recv_sem=halo_recv.at[n],
            device_id=device,
            device_id_type=MESH,
        )

    x_up = halo(0, x_last, x_low, on_x(1))
    x_down = halo(1, x_first, x_high, on_x(PX - 1))
    y_up = halo(2, y_last, y_low, on_y(1))
    y_down = halo(3, y_first, y_high, on_y(PY - 1))
    has_up, has_down = gx < PX - 1, gx > 0
    has_right, has_left = gy < PY - 1, gy > 0
    pl.when(has_up)(x_up.start)
    pl.when(has_down)(x_down.start)
    pl.when(has_right)(y_up.start)
    pl.when(has_left)(y_down.start)

    def spread(src, dst, n, along_x, size):
        peers, me = (PX, gx) if along_x else (PY, gy)
        mine = pl.ds(pl.multiple_of(me * size, 8), size)

        @pl.loop(1, peers)
        def _(d):
            device = on_x(d) if along_x else on_y(d)
            there = device[0] if along_x else device[1]
            pltpu.make_async_remote_copy(
                src_ref=src.at[pl.ds(pl.multiple_of(there * size, 8), size), :],
                dst_ref=dst.at[mine, :],
                send_sem=send_sem.at[n],
                recv_sem=recv_sem.at[n],
                device_id=device,
                device_id_type=MESH,
            ).start()

        dst[mine, :] = src[mine, :]

    def arrived(dst, n, peers, size):
        part = dst.at[pl.ds(0, (peers - 1) * size), :]
        pltpu.make_async_copy(part, part, recv_sem.at[n]).wait()

    def departed(src, n, peers, size):
        part = src.at[pl.ds(0, (peers - 1) * size), :]
        pltpu.make_async_copy(part, part, send_sem.at[n]).wait()

    spread(cxs, cxr, 0, True, 8)
    spread(cys, cyr, 1, False, 16)

    pl.when(has_down)(x_up.wait_recv)
    pl.when(has_up)(x_down.wait_recv)
    pl.when(has_left)(y_up.wait_recv)
    pl.when(has_right)(y_down.wait_recv)

    _, _, _, first_ref, last_ref = xf

    def source_row(k, sums):
        here = [fpad[f, k + 1, Y0 : Y0 + LY, :] for f in range(NF)]
        done = []
        for f in range(NF):
            across_x = fpad[f, k + 2, Y0 : Y0 + LY, :] - fpad[f, k, Y0 : Y0 + LY, :]
            across_y = (
                fpad[f, k + 1, Y0 + 1 : Y0 + LY + 1, :] - fpad[f, k + 1, Y0 - 1 : Y0 + LY - 1, :]
            )
            across_z = pltpu.roll(here[f], NZ - 1, 1) - pltpu.roll(here[f], 1, 1)
            carried = here[0] * across_x + here[1] * across_y + here[2] * across_z
            source = here[f] - (0.5 * ADVECT) * carried
            if f == 2:
                source = source + BUOYANT * here[3]
            cur[f, pl.ds(pl.multiple_of(k * LY, 8), LY), :] = source
            kind = KIND_OF[f]
            done.append(sums[f] + first_ref[kind, k] * source)
            done.append(sums[NF + f] + last_ref[kind, k] * source)
        return tuple(done[0::2] + done[1::2])

    zero = jnp.zeros((LY, NZ), jnp.float32)
    sums = lax.fori_loop(0, LX, source_row, (zero,) * (2 * NF))
    for r in range(8):
        xs[pl.ds(r, LY, stride=8), :] = sums[r]
    spread(xs, xr, 2, True, 8)

    inv_ref, low_ref, rat_ref, first_ref, last_ref = xf

    def x_rows(k):
        return pl.ds(pl.multiple_of(k * LY, 8), LY)

    def x_down_row(k, before):
        result = []
        for f in range(NF):
            kind = KIND_OF[f]
            value = inv_ref[kind, k] * cur[f, x_rows(k), :] + low_ref[kind, k] * before[f]
            inner[f, x_rows(k), :] = value
            result.append(value)
        return tuple(result)

    def x_up_row(step, after):
        k = LX - 3 - step
        result = []
        for f in range(NF):
            value = inner[f, x_rows(k), :] + rat_ref[KIND_OF[f], k] * after[f]
            inner[f, x_rows(k), :] = value
            result.append(value)
        return tuple(result)

    tail = lax.fori_loop(1, LX - 1, x_down_row, (zero,) * NF)
    lax.fori_loop(0, LX - 3, x_up_row, tail)

    arrived(cxr, 0, PX, 8)
    interface_factor(cxr, lambda b: 8 * b, PX, xi)
    arrived(cyr, 1, PY, 16)
    for t in range(2):
        interface_factor(cyr, lambda b, t=t: 16 * b + 8 * t, PY, yi[t])

    arrived(xr, 2, PX, 8)
    interface_solve(xr, xb, lambda b: 8 * b, PX, xi)
    spread(xb, xg, 3, True, 8)
    arrived(xg, 3, PX, 8)

    starts = [xg[pl.ds(f, LY, stride=8), :] for f in range(NF)]
    ends = [xg[pl.ds(NF + f, LY, stride=8), :] for f in range(NF)]
    for f in range(NF):
        cur[f, pl.ds(0, LY), :] = starts[f]
        cur[f, pl.ds((LX - 1) * LY, LY), :] = ends[f]

        @pl.loop(1, LX - 1)
        def _(k, f=f):
            kind = KIND_OF[f]
            cur[f, x_rows(k), :] = (
                inner[f, x_rows(k), :]
                + first_ref[kind, k] * starts[f]
                + last_ref[kind, k] * ends[f]
            )

    inv_ref, low_ref, rat_ref, first_ref, last_ref = yf

    def y_rows(k):
        return pl.ds(k, LX, stride=LY)

    zero = jnp.zeros((LX, NZ), jnp.float32)
    sums = [zero] * (2 * NF)
    for k in range(LY):
        for f in range(NF):
            kind = KIND_OF[f]
            value = cur[f, y_rows(k), :]
            if k < LY - 1:
                sums[f] = sums[f] + first_ref[kind, k] * value
            if k > 0:
                sums[NF + f] = sums[NF + f] + last_ref[kind, k] * value
    for r in range(8):
        ys[pl.ds(r, LX, stride=8), :] = sums[r]
    spread(ys, yr, 4, False, 16)

    before = [zero] * NF
    for k in range(1, LY - 1):
        for f in range(NF):
            kind = KIND_OF[f]
            before[f] = inv_ref[kind, k] * cur[f, y_rows(k), :] + low_ref[kind, k] * before[f]
            inner[f, pl.ds(k * LX, LX), :] = before[f]
    after = before
    for k in range(LY - 3, 0, -1):
        for f in range(NF):
            after[f] = inner[f, pl.ds(k * LX, LX), :] + rat_ref[KIND_OF[f], k] * after[f]
            inner[f, pl.ds(k * LX, LX), :] = after[f]

    arrived(yr, 4, PY, 16)
    for t in range(2):
        interface_solve(yr, yb, lambda b, t=t: 16 * b + 8 * t, PY, yi[t])
    spread(yb, yg, 5, False, 16)
    arrived(yg, 5, PY, 16)

    outs = []
    for f in range(NF):
        kind = KIND_OF[f]
        start, end = yg[pl.ds(f, LX, stride=8), :], yg[pl.ds(NF + f, LX, stride=8), :]
        outbuf[f, y_rows(0), :] = start
        outbuf[f, y_rows(LY - 1), :] = end
        for k in range(1, LY - 1):
            outbuf[f, y_rows(k), :] = (
                inner[f, pl.ds(k * LX, LX), :] + first_ref[kind, k] * start + last_ref[kind, k] * end
            )
        copy = pltpu.make_async_copy(outbuf.at[f], out.at[f], out_sem.at[f])
        copy.start()
        outs.append(copy)

    pl.when(has_up)(x_up.wait_send)
    pl.when(has_down)(x_down.wait_send)
    pl.when(has_right)(y_up.wait_send)
    pl.when(has_left)(y_down.wait_send)
    departed(cxs, 0, PX, 8)
    departed(cys, 1, PY, 16)
    departed(xs, 2, PX, 8)
    departed(xb, 3, PX, 8)
    departed(ys, 4, PY, 16)
    departed(yb, 5, PY, 16)
    for copy in outs:
        copy.wait()


def per_device(flow_state, viscosity):
    f32 = jnp.float32
    vmem = lambda *shape: pltpu.VMEM(shape, f32)
    rows = LX * LY
    result = pl.pallas_call(
        kernel,
        out_shape=jax.ShapeDtypeStruct((NF, rows, NZ), f32),
        in_specs=[pl.BlockSpec(memory_space=pl.ANY)] * 2,
        out_specs=pl.BlockSpec(memory_space=pl.ANY),
        scratch_shapes=[
            vmem(NF, LX + 2, LY + 16, NZ),
            vmem(rows, NZ),
            vmem(NF, rows, NZ),
            vmem(NF, rows, NZ),
            vmem(NF, rows, NZ),
            *[vmem(2, LX, LY, NZ)] * 5,
            *[vmem(2, LY, LX, NZ)] * 5,
            *[vmem(PX + 1, 8, NZ)] * 3,
            *[vmem(PY + 1, 8, NZ)] * 6,
            *[vmem(8 * PX, NZ)] * 2,
            *[vmem(16 * PY, NZ)] * 2,
            *[vmem(8 * PX, NZ)] * 4,
            *[vmem(16 * PY, NZ)] * 4,
            pltpu.SemaphoreType.DMA((2,)),
            pltpu.SemaphoreType.DMA((NF,)),
            pltpu.SemaphoreType.DMA((6,)),
            pltpu.SemaphoreType.DMA((6,)),
            pltpu.SemaphoreType.DMA((4,)),
            pltpu.SemaphoreType.DMA((4,)),
        ],
        compiler_params=pltpu.CompilerParams(collective_id=0, has_side_effects=True),
    )(flow_state, viscosity.reshape(rows, NZ))
    return result.reshape(NF, LX, LY, NZ)


def solution(mesh):
    return jax.shard_map(
        per_device,
        mesh=mesh,
        in_specs=(P(None, "gx", "gy", None), P("gx", "gy", None)),
        out_specs=P(None, "gx", "gy", None),
        check_vma=False,
    )
```

time: 165 us -> 43.2 us (0.26); the launches traced: 163 us -> 43 us
  starting transfers between devices: 63.8 us -> 0 us
  Pallas kernels: 0 us -> 40.8 us
  other arithmetic: 32.9 us -> 0 us
  waiting for transfers between devices: 27.3 us -> 0 us
  local copies, waits for them, and re-layouts: 29.2 us -> 2.26 us
  blocking collectives: 8 us -> 0 us
  between operations: 2.04 us -> 0.01 us
    pallas_call x0 -> x1, Pallas kernels: none -> 40.8 us  [per_device(): pl.pallas_call(kernel, out_shape=jax.ShapeDtypeStruct((NF, rows, NZ), f32...]
    all_to_all x6 -> x0, starting transfers between devices: 40.3 us -> none  [the longest x1 13.6 us: solve_along_x(): lax.all_to_all(packed, GX, split_axis=1, concat_axis=0, tiled=True)]
    all_to_all x6 -> x0, waiting for transfers between devices: 27.3 us -> none  [the longest x2 10.8 us: exchange_in_order(): result = lax.all_to_all(result, axes[k], k, k, tiled=True)]
    ppermute x8 -> x0, starting transfers between devices: 23.5 us -> none  [the longest x4 17.1 us: padded_2(): lax.ppermute(last, axis, up)]
    slice x26 -> x0, local copies, waits for them, and re-layouts: 11.8 us -> none  [the longest x2 3.39 us: advect(): along_z = 0.5 * (jnp.roll(flow_state, -1, 3) - jnp.roll(flow_state, 1, 3))]
    mul x13 -> x0, other arithmetic: 8.85 us -> none  [the longest x4 3.97 us: sweep_down(): forward.append(running * inverse[k])]
    all_to_all x1 -> x0, blocking collectives: 8 us -> none  [solve_along_y(): lax.all_to_all(solution, 'gy', split_axis=0, concat_axis=1, tiled=True)]
    unnamed x82 -> x0, other arithmetic: 7.85 us -> none
  transfers between devices with their start and end apart: 14 -> 0, of which waited for: 5 -> 0; matrix products, arithmetic and copies ran while one was open for 21% -> 0% of each run, Pallas kernels for 0% -> 0%
where the time goes in v1:
time: 43.2 us; the launch traced here: 43 us
  Pallas kernels  40.8 us (94%)
  local copies, waits for them, and re-layouts  2.26 us (5%)
    pallas_call x1, Pallas kernels, per_device(): pl.pallas_call(kernel, out_shape=jax.ShapeDtypeStruct((NF, rows, NZ), f32...  40.8 us
    unnamed x1, local copies, waits for them, and re-layouts  2.26 us

profile of v1, /device:TPU:1, one launch (start us, length us, event | category | flops | bytes accessed | tf_op | source)
XLA Modules:
  0.0 43.0 jit_solution(6356625085569553518)
XLA Ops:
  0.0 40.8 %shard_map.28 = f32[4,512,128]{2,1,0:T(8,128)} custom-call(f32[4,16,32,128]{3,2,1,0:T(8,128)} %flow.1, f32[512,128]{1,0:T(8,128)} %bitcast.3), custom_call_target="tpu_custom_call" | custom-call | tf_op jit(solution)/shard_map/pallas_call | solution.py:418
  40.8 2.3 %copy.4 = f32[4,16,32,128]{3,2,1,0:T(8,128)} copy(f32[4,16,32,128]{3,2,1,0:T(8,128)} %bitcast.2) | data formatting | bytes 2097152

commit v2 on v1

v2 whole, which is shorter than its diff:
```python
import jax
import jax.numpy as jnp
from jax import lax
from jax.experimental import pallas as pl
from jax.experimental.pallas import tpu as pltpu
from jax.sharding import PartitionSpec as P

MESH = pl.DeviceIdType.MESH

ADVECT = 0.2
BUOYANT = 0.5
CONDUCT = 0.6
KINDS = (1.0, CONDUCT)
KIND_OF = (0, 0, 0, 1)

NF = 4
LX, LY, NZ = 16, 32, 128
PX, PY = 32, 8
Y0 = 8


def factor(faces, along):
    inverse, lower, ratio = {}, {}, {}
    one = jnp.ones_like(faces[1])
    running = one
    forward = {}
    for k in range(1, along - 1):
        centre = 1.0 + faces[k] + faces[k + 1]
        if k > 1:
            centre = centre - faces[k] * ratio[k - 1]
        inverse[k] = 1.0 / centre
        lower[k] = faces[k] * inverse[k]
        ratio[k] = faces[k + 1] * inverse[k]
        running = lower[k] * running
        forward[k] = running
    first, last = {along - 1: jnp.zeros_like(one)}, {along - 1: one}
    for k in range(along - 2, 0, -1):
        first[k] = forward[k] + ratio[k] * first[k + 1]
        last[k] = ratio[k] * last[k + 1]
    first[0], last[0] = one, jnp.zeros_like(one)
    return inverse, lower, ratio, first, last


def keep_factor(load, along, keep, keep_ends, tiles):
    cells = [load(k) for k in range(along)]
    middles = [None] + [cells[k - 1] + cells[k] for k in range(1, along)]
    tiles[0] = cells[0]
    tiles[1] = cells[-1]
    for kind, scale in enumerate(KINDS):
        faces = [None] + [(0.5 * scale) * m for m in middles[1:]]
        inverse, lower, ratio, first, last = factor(faces, along)
        for k in range(1, along - 1):
            keep(kind, k, inverse[k], lower[k], ratio[k])
        for k in range(along):
            keep_ends(kind, k, first[k], last[k])
        tiles[2 + kind] = 1.0 + faces[1] * (1.0 - first[1])
        tiles[4 + kind] = faces[1] * last[1]
        tiles[6 + kind] = 1.0 + faces[along - 1] * (1.0 - last[along - 2])


def rolled(value):
    return pltpu.roll(value, 4, 0)


def interface_factor(coef, base, blocks, refs):
    inv_ref, low_ref, rat_ref = refs
    sub = lax.broadcasted_iota(jnp.int32, (8, NZ), 0)
    down = sub < 4
    thermal = (sub == 3) | (sub == 7)

    def row(block, r):
        return jnp.broadcast_to(coef[pl.ds(base(block) + r, 1), :], (8, NZ))

    def by_kind(block, r):
        return jnp.where(thermal, row(block, r + 1), row(block, r))

    scale = jnp.where(thermal, CONDUCT, 1.0).astype(jnp.float32)
    half = blocks // 2
    sides = []
    for i in range(half + 1):
        if i == 0:
            value = jnp.where(down, row(0, 0), row(blocks - 1, 1))
        elif i == half:
            value = 0.5 * (row(i - 1, 1) + row(i, 0))
        else:
            value = 0.5 * jnp.where(
                down,
                row(i - 1, 1) + row(i, 0),
                row(blocks - 1 - i, 1) + row(blocks - i, 0),
            )
        sides.append(scale * value)
    ratio = None
    for i in range(half):
        j = blocks - 1 - i
        couple = jnp.where(down, by_kind(i, 4), by_kind(j, 4))
        even = jnp.where(down, by_kind(i, 2), by_kind(j, 6)) + sides[i]
        odd = jnp.where(down, by_kind(i, 6), by_kind(j, 2)) + sides[i + 1]
        for m, centre, before, after in (
            (2 * i, even, sides[i], couple),
            (2 * i + 1, odd, couple, sides[i + 1]),
        ):
            if m > 0:
                centre = centre - before * ratio
            inverse = 1.0 / centre
            ratio = after * inverse
            inv_ref[m] = inverse
            low_ref[m] = before * inverse
            rat_ref[m] = ratio
    inv_ref[blocks] = 1.0 / (1.0 - ratio * rolled(ratio))


def interface_solve(right, solved, base, blocks, refs):
    inv_ref, low_ref, rat_ref = refs
    down = lax.broadcasted_iota(jnp.int32, (8, NZ), 0) < 4
    half = blocks // 2
    forward = []
    for i in range(half):
        j = blocks - 1 - i
        mine, other = right[pl.ds(base(i), 8), :], right[pl.ds(base(j), 8), :]
        even = jnp.where(down, mine, other)
        odd = rolled(jnp.where(down, other, mine))
        for m, value in ((2 * i, even), (2 * i + 1, odd)):
            value = inv_ref[m] * value
            if m > 0:
                value = value + low_ref[m] * forward[-1]
            forward.append(value)
    tail = forward[-1]
    values = [None] * blocks
    values[-1] = (tail + rat_ref[blocks - 1] * rolled(tail)) * inv_ref[blocks]
    for m in range(blocks - 2, -1, -1):
        values[m] = forward[m] + rat_ref[m] * values[m + 1]
    for i in range(half):
        j = blocks - 1 - i
        even, odd = values[2 * i], rolled(values[2 * i + 1])
        solved[pl.ds(base(i), 8), :] = jnp.where(down, even, odd)
        solved[pl.ds(base(j), 8), :] = jnp.where(down, odd, even)


def far_first(size_a, size_b):
    hops = lambda d, size: min(d, size - d)
    offsets = [(a, b) for a in range(size_a) for b in range(size_b) if (a, b) != (0, 0)]
    return sorted(offsets, key=lambda o: -hops(o[0], size_a) - hops(o[1], size_b))


def kernel(flow, visc, inner_y, first_y, last_y, yg, flat, vbuf, cur, inner, part, *rest):
    inv_x, low_x, rat_x, first_x, last_x = rest[0:5]
    inv_y, low_y, rat_y = rest[5:8]
    xi, yi = rest[8:11], (rest[11:14], rest[14:17])
    cxs, cxr, cys, cyr, xs, xr, xb, xg, ys, yr, yb = rest[17:28]
    xh_low, xh_high, yh_low, yh_high = rest[28:32]
    in_sem, send_sem, recv_sem, halo_send, halo_recv = rest[32:]
    gx, gy = lax.axis_index("gx"), lax.axis_index("gy")

    barrier = pltpu.get_barrier_semaphore()
    ring_z, cores = 8, 2
    ring_x, ring_y = PX // ring_z, PY // cores
    cx, cz = lax.div(gx, ring_z), lax.rem(gx, ring_z)
    cy, cc = lax.div(gy, cores), lax.rem(gy, cores)
    x_peers = [
        lax.rem(cx + dx, ring_x) * ring_z + lax.rem(cz + dz, ring_z)
        for dx, dz in far_first(ring_x, ring_z)
    ]
    y_peers = [
        lax.rem(cy + dy, ring_y) * cores + lax.rem(cc + dc, cores)
        for dy, dc in far_first(ring_y, cores)
    ]
    for peer in x_peers:
        pl.semaphore_signal(barrier, inc=1, device_id=(peer, gy), device_id_type=MESH)
    for peer in y_peers:
        pl.semaphore_signal(barrier, inc=1, device_id=(gx, peer), device_id_type=MESH)

    visc_in = pltpu.make_async_copy(visc, vbuf, in_sem.at[0])
    visc_in.start()
    wide = LY + 16

    def cells(k, shift=0):
        return pl.ds((k + 1) * wide + Y0 + shift, LY)

    flow_in = [
        pltpu.make_async_copy(flow.at[:, k], flat.at[:, cells(k), :], in_sem.at[1 + k])
        for k in range(LX)
    ]
    for copy in flow_in:
        copy.start()

    slab, edge = jnp.zeros((LY, NZ), jnp.float32), jnp.zeros((LX, NZ), jnp.float32)
    for f in range(NF):
        flat[f, cells(-1), :] = slab
        flat[f, cells(LX), :] = slab
        flat[f, pl.ds(wide + Y0 - 1, LX, stride=wide), :] = edge
        flat[f, pl.ds(wide + Y0 + LY, LX, stride=wide), :] = edge
        inner[f, pl.ds(0, LY), :] = slab
        inner[f, pl.ds((LX - 1) * LY, LY), :] = slab
        inner_y[f, pl.ds(0, LX, stride=LY), :] = edge
        inner_y[f, pl.ds(LY - 1, LX, stride=LY), :] = edge

    has_up, has_down = gx < PX - 1, gx > 0
    has_right, has_left = gy < PY - 1, gy > 0

    @pl.when(gx == 0)
    def _():
        xh_low[...] = jnp.zeros_like(xh_low)

    @pl.when(gx == PX - 1)
    def _():
        xh_high[...] = jnp.zeros_like(xh_high)

    @pl.when(gy == 0)
    def _():
        yh_low[...] = jnp.zeros_like(yh_low)

    @pl.when(gy == PY - 1)
    def _():
        yh_high[...] = jnp.zeros_like(yh_high)

    def x_rows(k):
        return pl.ds(pl.multiple_of(k * LY, 8), LY)

    def y_rows(k):
        return pl.ds(k, LX, stride=LY)

    def keep_x(kind, k, inverse, lower, ratio):
        inv_x[kind, x_rows(k), :] = inverse
        low_x[kind, x_rows(k), :] = lower
        rat_x[kind, x_rows(k), :] = ratio

    def keep_x_ends(kind, k, first, last):
        first_x[kind, x_rows(k), :] = first
        last_x[kind, x_rows(k), :] = last

    def keep_y(kind, k, inverse, lower, ratio):
        inv_y[kind, pl.ds(k * LX, LX), :] = inverse
        low_y[kind, pl.ds(k * LX, LX), :] = lower
        rat_y[kind, pl.ds(k * LX, LX), :] = ratio

    def keep_y_ends(kind, k, first, last):
        first_y[kind, y_rows(k), :] = first
        last_y[kind, y_rows(k), :] = last

    visc_in.wait()
    tiles = {}
    keep_factor(lambda k: vbuf[x_rows(k), :], LX, keep_x, keep_x_ends, tiles)
    for r in range(8):
        cxs[pl.ds(r, LY, stride=8), :] = tiles[r]

    for copy in flow_in:
        copy.wait()
    pl.semaphore_wait(barrier, PX - 1 + PY - 1)

    def halo(n, src, dst, device):
        return pltpu.make_async_remote_copy(
            src_ref=src,
            dst_ref=dst,
            send_sem=halo_send.at[n],
            recv_sem=halo_recv.at[n],
            device_id=device,
            device_id_type=MESH,
        )

    x_up = halo(0, flat.at[:, cells(LX - 1), :], xh_low, (lax.rem(gx + 1, PX), gy))
    x_down = halo(1, flat.at[:, cells(0), :], xh_high, (lax.rem(gx + PX - 1, PX), gy))
    y_up = halo(2, flow.at[:, :, LY - 1, :], yh_low, (gx, lax.rem(gy + 1, PY)))
    y_down = halo(3, flow.at[:, :, 0, :], yh_high, (gx, lax.rem(gy + PY - 1, PY)))
    pl.when(has_up)(x_up.start)
    pl.when(has_down)(x_down.start)
    pl.when(has_right)(y_up.start)
    pl.when(has_left)(y_down.start)

    def spread(src, dst, n, along_x, size):
        peers, me = (x_peers, gx) if along_x else (y_peers, gy)
        mine = pl.ds(pl.multiple_of(me * size, 8), size)
        for peer in peers:
            pltpu.make_async_remote_copy(
                src_ref=src.at[pl.ds(pl.multiple_of(peer * size, 8), size), :],
                dst_ref=dst.at[mine, :],
                send_sem=send_sem.at[n],
                recv_sem=recv_sem.at[n],
                device_id=(peer, gy) if along_x else (gx, peer),
                device_id_type=MESH,
            ).start()
        dst[mine, :] = src[mine, :]

    def arrived(dst, n, peers, size):
        piece = dst.at[pl.ds(0, (peers - 1) * size), :]
        pltpu.make_async_copy(piece, piece, recv_sem.at[n]).wait()

    def departed(src, n, peers, size):
        piece = src.at[pl.ds(0, (peers - 1) * size), :]
        pltpu.make_async_copy(piece, piece, send_sem.at[n]).wait()

    spread(cxs, cxr, 0, True, 8)

    def source_row(k, sums):
        here = [flat[f, cells(k), :] for f in range(NF)]
        firsts, lasts = [], []
        for f in range(NF):
            across_x = flat[f, cells(k + 1), :] - flat[f, cells(k - 1), :]
            across_y = flat[f, cells(k, 1), :] - flat[f, cells(k, -1), :]
            across_z = pltpu.roll(here[f], NZ - 1, 1) - pltpu.roll(here[f], 1, 1)
            carried = here[0] * across_x + here[1] * across_y + here[2] * across_z
            source = here[f] - (0.5 * ADVECT) * carried
            if f == 2:
                source = source + BUOYANT * here[3]
            cur[f, x_rows(k), :] = source
            kind = KIND_OF[f]
            firsts.append(sums[f] + first_x[kind, x_rows(k), :] * source)
            lasts.append(sums[NF + f] + last_x[kind, x_rows(k), :] * source)
        return tuple(firsts + lasts)

    sums = (slab,) * (2 * NF)
    for k in range(LX):
        sums = source_row(k, sums)
    for r in range(8):
        xs[pl.ds(r, LY, stride=8), :] = sums[r]

    tiles = {}
    keep_factor(lambda k: vbuf[y_rows(k), :], LY, keep_y, keep_y_ends, tiles)
    for r in range(8):
        cys[pl.ds(r, LX, stride=8), :] = tiles[r]
    spread(cys, cyr, 1, False, 16)

    half = 0.5 * ADVECT
    pl.when(has_left)(y_up.wait_recv)
    pl.when(has_right)(y_down.wait_recv)
    for at, around, sign in ((0, yh_low, half), (LY - 1, yh_high, -half)):
        speed = sign * flat[1, pl.ds(wide + Y0 + at, LX, stride=wide), :]
        for f in range(NF):
            kind = KIND_OF[f]
            change = speed * around[f]
            cur[f, y_rows(at), :] = cur[f, y_rows(at), :] + change
            for r, weight in ((f, first_x), (NF + f, last_x)):
                row = pl.ds(at * 8 + r, 1)
                total = jnp.sum(weight[kind, y_rows(at), :] * change, axis=0, keepdims=True)
                xs[row, :] = xs[row, :] + total
    pl.when(has_down)(x_up.wait_recv)
    pl.when(has_up)(x_down.wait_recv)
    for r, at, around, sign in ((0, 0, xh_low, half), (NF, LX - 1, xh_high, -half)):
        speed = sign * flat[0, cells(at), :]
        for f in range(NF):
            row = pl.ds(r + f, LY, stride=8)
            xs[row, :] = xs[row, :] + speed * around[f]
    spread(xs, xr, 2, True, 8)

    def x_down_row(k, before):
        result = []
        for f in range(NF):
            kind = KIND_OF[f]
            value = inv_x[kind, x_rows(k), :] * cur[f, x_rows(k), :] + low_x[kind, x_rows(k), :] * before[f]
            inner[f, x_rows(k), :] = value
            result.append(value)
        return tuple(result)

    def x_up_row(step, after):
        k = LX - 3 - step
        result = []
        for f in range(NF):
            value = inner[f, x_rows(k), :] + rat_x[KIND_OF[f], x_rows(k), :] * after[f]
            inner[f, x_rows(k), :] = value
            result.append(value)
        return tuple(result)

    tail = lax.fori_loop(1, LX - 1, x_down_row, (slab,) * NF)
    lax.fori_loop(0, LX - 3, x_up_row, tail)

    arrived(cxr, 0, PX, 8)
    interface_factor(cxr, lambda b: 8 * b, PX, xi)
    arrived(cyr, 1, PY, 16)
    for t in range(2):
        interface_factor(cyr, lambda b, t=t: 16 * b + 8 * t, PY, yi[t])

    arrived(xr, 2, PX, 8)
    interface_solve(xr, xb, lambda b: 8 * b, PX, xi)
    spread(xb, xg, 3, True, 8)
    arrived(xg, 3, PX, 8)

    for f in range(NF):
        kind = KIND_OF[f]
        start, end = xg[pl.ds(f, LY, stride=8), :], xg[pl.ds(NF + f, LY, stride=8), :]

        def x_row(k, carry, f=f, kind=kind, start=start, end=end):
            rows = x_rows(k)
            value = inner[f, rows, :] + first_x[kind, rows, :] * start + last_x[kind, rows, :] * end
            cur[f, rows, :] = value
            for r, weight in ((f, first_y), (NF + f, last_y)):
                share = weight[kind, rows, :] * value
                total = share[0:8]
                for q in range(8, LY, 8):
                    total = total + share[q : q + 8]
                part[pl.ds(pl.multiple_of(k * 64, 8) + 8 * r, 8), :] = total
            return carry

        lax.fori_loop(0, LX, x_row, 0, unroll=4)
    for k in range(LX):
        total = part[pl.ds(64 * k, 8, stride=8), :]
        for q in range(1, 8):
            total = total + part[pl.ds(64 * k + q, 8, stride=8), :]
        ys[pl.ds(8 * k, 8), :] = total
    spread(ys, yr, 4, False, 16)

    before = [edge] * NF
    for k in range(1, LY - 1):
        rows = pl.ds(k * LX, LX)
        for f in range(NF):
            kind = KIND_OF[f]
            before[f] = inv_y[kind, rows, :] * cur[f, y_rows(k), :] + low_y[kind, rows, :] * before[f]
            inner[f, rows, :] = before[f]
    after = before
    for f in range(NF):
        inner_y[f, y_rows(LY - 2), :] = after[f]
    for k in range(LY - 3, 0, -1):
        rows = pl.ds(k * LX, LX)
        for f in range(NF):
            after[f] = inner[f, rows, :] + rat_y[KIND_OF[f], rows, :] * after[f]
            inner_y[f, y_rows(k), :] = after[f]

    arrived(yr, 4, PY, 16)
    for t in range(2):
        interface_solve(yr, yb, lambda b, t=t: 16 * b + 8 * t, PY, yi[t])
    spread(yb, yg, 5, False, 16)

    pl.when(has_up)(x_up.wait_send)
    pl.when(has_down)(x_down.wait_send)
    pl.when(has_right)(y_up.wait_send)
    pl.when(has_left)(y_down.wait_send)
    departed(cxs, 0, PX, 8)
    departed(cys, 1, PY, 16)
    departed(xs, 2, PX, 8)
    departed(xb, 3, PX, 8)
    departed(ys, 4, PY, 16)
    departed(yb, 5, PY, 16)
    arrived(yg, 5, PY, 16)


CHUNK = 4


def assemble(inner, first, last, ends, out, done, sem):
    copies = []
    for k in range(LX):
        rows = pl.ds(k * LY, LY)
        for f in range(NF):
            kind = KIND_OF[f]
            done[f, rows, :] = (
                inner[f, rows, :]
                + first[kind, rows, :] * ends[pl.ds(8 * k + f, 1), :]
                + last[kind, rows, :] * ends[pl.ds(8 * k + NF + f, 1), :]
            )
        if k % CHUNK == CHUNK - 1:
            rows = pl.ds((k + 1 - CHUNK) * LY, CHUNK * LY)
            copies.append(
                pltpu.make_async_copy(done.at[:, rows, :], out.at[:, rows, :], sem.at[k // CHUNK])
            )
            copies[-1].start()
    for copy in copies:
        copy.wait()


def per_device(flow_state, viscosity):
    f32 = jnp.float32
    vmem = lambda *shape: pltpu.VMEM(shape, f32)
    rows = LX * LY
    in_vmem = pl.BlockSpec(memory_space=pltpu.VMEM)
    kept = pl.pallas_call(
        kernel,
        out_shape=[
            vmem(NF, rows, NZ),
            vmem(2, rows, NZ),
            vmem(2, rows, NZ),
            vmem(16 * PY, NZ),
        ],
        in_specs=[pl.BlockSpec(memory_space=pl.ANY)] * 2,
        out_specs=[in_vmem] * 4,
        scratch_shapes=[
            vmem(NF, (LX + 2) * (LY + 16), NZ),
            vmem(rows, NZ),
            vmem(NF, rows, NZ),
            vmem(NF, rows, NZ),
            vmem(LX * 64, NZ),
            *[vmem(2, rows, NZ)] * 8,
            *[vmem(PX + 1, 8, NZ)] * 3,
            *[vmem(PY + 1, 8, NZ)] * 6,
            *[vmem(8 * PX, NZ)] * 2,
            *[vmem(16 * PY, NZ)] * 2,
            *[vmem(8 * PX, NZ)] * 4,
            *[vmem(16 * PY, NZ)] * 3,
            *[vmem(NF, LY, NZ)] * 2,
            *[vmem(NF, LX, NZ)] * 2,
            pltpu.SemaphoreType.DMA((1 + LX,)),
            pltpu.SemaphoreType.DMA((6,)),
            pltpu.SemaphoreType.DMA((6,)),
            pltpu.SemaphoreType.DMA((4,)),
            pltpu.SemaphoreType.DMA((4,)),
        ],
        compiler_params=pltpu.CompilerParams(collective_id=0, has_side_effects=True),
    )(flow_state, viscosity.reshape(rows, NZ))
    result = pl.pallas_call(
        assemble,
        out_shape=jax.ShapeDtypeStruct((NF, rows, NZ), f32),
        in_specs=[in_vmem] * 4,
        out_specs=pl.BlockSpec(memory_space=pl.ANY),
        scratch_shapes=[vmem(NF, rows, NZ), pltpu.SemaphoreType.DMA((LX // CHUNK,))],
        compiler_params=pltpu.CompilerParams(vmem_limit_bytes=8 << 20),
    )(*kept)
    return result.reshape(NF, LX, LY, NZ)


def solution(mesh):
    return jax.shard_map(
        per_device,
        mesh=mesh,
        in_specs=(P(None, "gx", "gy", None), P("gx", "gy", None)),
        out_specs=P(None, "gx", "gy", None),
        check_vma=False,
    )
```

time: 43.2 us -> 36.9 us (0.85)
  Pallas kernels: 40.8 us -> 36.8 us
  local copies, waits for them, and re-layouts: 2.26 us -> 0 us
    pallas_call x1 -> x2, Pallas kernels: 40.8 us -> 36.8 us  [the longest x1 35.7 us: per_device(): pl.pallas_call(kernel, out_shape=[vmem(NF, rows, NZ), vmem(2, rows, NZ),...]
    unnamed x1 -> x0, local copies, waits for them, and re-layouts: 2.26 us -> none
where the time goes in v2:
time: 36.9 us; the launch traced here: 36.8 us
  Pallas kernels  36.8 us (100%)
    pallas_call x1, Pallas kernels, per_device(): pl.pallas_call(kernel, out_shape=[vmem(NF, rows, NZ), vmem(2, rows, NZ),...  35.7 us
    pallas_call x1, Pallas kernels, per_device(): pl.pallas_call(assemble, out_shape=jax.ShapeDtypeStruct((NF, rows, NZ), f...  1.04 us

profile of v2, /device:TPU:1, one launch (start us, length us, event | category | flops | bytes accessed | tf_op | source)
XLA Modules:
  0.0 36.8 jit_solution(12687805004832985937)
XLA Ops:
  0.0 35.7 %shard_map.28 = (f32[4,512,128]{2,1,0:T(8,128)S(1)}, f32[2,512,128]{2,1,0:T(8,128)S(1)}, f32[2,512,128]{2,1,0:T(8,128)S(1)}, f32[128,128]{1,0:T(8,128)S(1)}) custom-call(f32[4,16,32,128]{3,2,1,0:T(8,128)} %flow.1, f32[512,128]{1,0:T(8,128)} %bitcast.2), custom_call_target="tpu_custom_call" | custom-call | tf_op jit(solution)/shard_map/pallas_call | solution.py:463
  35.7 1.0 %shard_map.29 = f32[4,512,128]{2,1,0:T(8,128)} custom-call(f32[4,512,128]{2,1,0:T(8,128)S(1)} %get-tuple-element.9.inner, f32[2,512,128]{2,1,0:T(8,128)S(1)} %get-tuple-element.10.first, f32[2,512,128]{2,1,0:T(8,128)S(1)} %get-tuple-element.11.last, f32[128,128]{1,0:T(8,128)S(1)} %get-tuple-element.12.ends), custom_call_target="tpu_custom_call" | custom-call | tf_op jit(solution)/shard_map/pallas_call | solution.py:496

commit v3 on v2

--- a/solution.py
+++ b/solution.py
@@ -17,6 +17,7 @@
 LX, LY, NZ = 16, 32, 128
 PX, PY = 32, 8
 Y0 = 8
+STAGES = 6
 
 
 def factor(faces, along):
@@ -137,9 +138,13 @@
 
 
 def far_first(size_a, size_b):
-    hops = lambda d, size: min(d, size - d)
-    offsets = [(a, b) for a in range(size_a) for b in range(size_b) if (a, b) != (0, 0)]
-    return sorted(offsets, key=lambda o: -hops(o[0], size_a) - hops(o[1], size_b))
+    hops = lambda a, b: min(a, size_a - a) + min(b, size_b - b)
+    offsets = [(a, b, hops(a, b)) for a in range(size_a) for b in range(size_b) if (a, b) != (0, 0)]
+    return sorted(offsets, key=lambda o: -o[2])
+
+
+def beside(size):
+    return sorted({1 % size, size - 1} - {0})
 
 
 def kernel(flow, visc, inner_y, first_y, last_y, yg, flat, vbuf, cur, inner, part, *rest):
@@ -148,7 +153,7 @@
     xi, yi = rest[8:11], (rest[11:14], rest[14:17])
     cxs, cxr, cys, cyr, xs, xr, xb, xg, ys, yr, yb = rest[17:28]
     xh_low, xh_high, yh_low, yh_high = rest[28:32]
-    in_sem, send_sem, recv_sem, halo_send, halo_recv = rest[32:]
+    in_sem, send_sem, recv_sem, halo_send, halo_recv, meet = rest[32:]
     gx, gy = lax.axis_index("gx"), lax.axis_index("gy")
 
     barrier = pltpu.get_barrier_semaphore()
@@ -157,17 +162,44 @@
     cx, cz = lax.div(gx, ring_z), lax.rem(gx, ring_z)
     cy, cc = lax.div(gy, cores), lax.rem(gy, cores)
     x_peers = [
-        lax.rem(cx + dx, ring_x) * ring_z + lax.rem(cz + dz, ring_z)
-        for dx, dz in far_first(ring_x, ring_z)
+        (lax.rem(cx + dx, ring_x) * ring_z + lax.rem(cz + dz, ring_z), hops)
+        for dx, dz, hops in far_first(ring_x, ring_z)
     ]
     y_peers = [
-        lax.rem(cy + dy, ring_y) * cores + lax.rem(cc + dc, cores)
-        for dy, dc in far_first(ring_y, cores)
+        (lax.rem(cy + dy, ring_y) * cores + lax.rem(cc + dc, cores), hops)
+        for dy, dc, hops in far_first(ring_y, cores)
     ]
-    for peer in x_peers:
-        pl.semaphore_signal(barrier, inc=1, device_id=(peer, gy), device_id_type=MESH)
-    for peer in y_peers:
-        pl.semaphore_signal(barrier, inc=1, device_id=(gx, peer), device_id_type=MESH)
+    up, down = (lax.rem(gx + 1, PX), gy), (lax.rem(gx + PX - 1, PX), gy)
+    right, left = (gx, lax.rem(gy + 1, PY)), (gx, lax.rem(gy + PY - 1, PY))
+    has_up, has_down = gx < PX - 1, gx > 0
+    has_right, has_left = gy < PY - 1, gy > 0
+
+    neighbours = (
+        [(cx * ring_z + lax.rem(cz + d, ring_z), gy) for d in beside(ring_z)]
+        + [(lax.rem(cx + d, ring_x) * ring_z + cz, gy) for d in beside(ring_x)]
+        + [(gx, lax.rem(gy + d, PY)) for d in beside(PY)]
+    )
+    crosses_up = has_up & (cz == ring_z - 1)
+    crosses_down = has_down & (cz == 0)
+
+    def greet(sem):
+        for device in neighbours:
+            pl.semaphore_signal(sem, inc=1, device_id=device, device_id_type=MESH)
+
+    def met(stage):
+        pl.semaphore_wait(meet.at[stage - 2], len(neighbours))
+        if stage < STAGES:
+            greet(meet.at[stage - 1])
+
+    greet(barrier)
+
+    @pl.when(crosses_up)
+    def _():
+        pl.semaphore_signal(barrier, inc=1, device_id=up, device_id_type=MESH)
+
+    @pl.when(crosses_down)
+    def _():
+        pl.semaphore_signal(barrier, inc=1, device_id=down, device_id_type=MESH)
 
     visc_in = pltpu.make_async_copy(visc, vbuf, in_sem.at[0])
     visc_in.start()
@@ -194,9 +226,6 @@
         inner_y[f, pl.ds(0, LX, stride=LY), :] = edge
         inner_y[f, pl.ds(LY - 1, LX, stride=LY), :] = edge
 
-    has_up, has_down = gx < PX - 1, gx > 0
-    has_right, has_left = gy < PY - 1, gy > 0
-
     @pl.when(gx == 0)
     def _():
         xh_low[...] = jnp.zeros_like(xh_low)
@@ -213,39 +242,8 @@
     def _():
         yh_high[...] = jnp.zeros_like(yh_high)
 
-    def x_rows(k):
-        return pl.ds(pl.multiple_of(k * LY, 8), LY)
-
-    def y_rows(k):
-        return pl.ds(k, LX, stride=LY)
-
-    def keep_x(kind, k, inverse, lower, ratio):
-        inv_x[kind, x_rows(k), :] = inverse
-        low_x[kind, x_rows(k), :] = lower
-        rat_x[kind, x_rows(k), :] = ratio
-
-    def keep_x_ends(kind, k, first, last):
-        first_x[kind, x_rows(k), :] = first
-        last_x[kind, x_rows(k), :] = last
-
-    def keep_y(kind, k, inverse, lower, ratio):
-        inv_y[kind, pl.ds(k * LX, LX), :] = inverse
-        low_y[kind, pl.ds(k * LX, LX), :] = lower
-        rat_y[kind, pl.ds(k * LX, LX), :] = ratio
-
-    def keep_y_ends(kind, k, first, last):
-        first_y[kind, y_rows(k), :] = first
-        last_y[kind, y_rows(k), :] = last
-
-    visc_in.wait()
-    tiles = {}
-    keep_factor(lambda k: vbuf[x_rows(k), :], LX, keep_x, keep_x_ends, tiles)
-    for r in range(8):
-        cxs[pl.ds(r, LY, stride=8), :] = tiles[r]
-
-    for copy in flow_in:
-        copy.wait()
-    pl.semaphore_wait(barrier, PX - 1 + PY - 1)
+    crossings = crosses_up.astype(jnp.int32) + crosses_down.astype(jnp.int32)
+    pl.semaphore_wait(barrier, len(neighbours) + crossings)
 
     def halo(n, src, dst, device):
         return pltpu.make_async_remote_copy(
@@ -257,28 +255,61 @@
             device_id_type=MESH,
         )
 
-    x_up = halo(0, flat.at[:, cells(LX - 1), :], xh_low, (lax.rem(gx + 1, PX), gy))
-    x_down = halo(1, flat.at[:, cells(0), :], xh_high, (lax.rem(gx + PX - 1, PX), gy))
-    y_up = halo(2, flow.at[:, :, LY - 1, :], yh_low, (gx, lax.rem(gy + 1, PY)))
-    y_down = halo(3, flow.at[:, :, 0, :], yh_high, (gx, lax.rem(gy + PY - 1, PY)))
+    x_up = halo(0, flow.at[:, LX - 1], xh_low, up)
+    x_down = halo(1, flow.at[:, 0], xh_high, down)
+    y_up = halo(2, flow.at[:, :, LY - 1, :], yh_low, right)
+    y_down = halo(3, flow.at[:, :, 0, :], yh_high, left)
     pl.when(has_up)(x_up.start)
     pl.when(has_down)(x_down.start)
     pl.when(has_right)(y_up.start)
     pl.when(has_left)(y_down.start)
-
-    def spread(src, dst, n, along_x, size):
+    greet(meet.at[0])
+
+    def x_rows(k):
+        return pl.ds(pl.multiple_of(k * LY, 8), LY)
+
+    def y_rows(k):
+        return pl.ds(k, LX, stride=LY)
+
+    def keep_x(kind, k, inverse, lower, ratio):
+        inv_x[kind, x_rows(k), :] = inverse
+        low_x[kind, x_rows(k), :] = lower
+        rat_x[kind, x_rows(k), :] = ratio
+
+    def keep_x_ends(kind, k, first, last):
+        first_x[kind, x_rows(k), :] = first
+        last_x[kind, x_rows(k), :] = last
+
+    def keep_y(kind, k, inverse, lower, ratio):
+        inv_y[kind, pl.ds(k * LX, LX), :] = inverse
+        low_y[kind, pl.ds(k * LX, LX), :] = lower
+        rat_y[kind, pl.ds(k * LX, LX), :] = ratio
+
+    def keep_y_ends(kind, k, first, last):
+        first_y[kind, y_rows(k), :] = first
+        last_y[kind, y_rows(k), :] = last
+
+    visc_in.wait()
+    tiles = {}
+    keep_factor(lambda k: vbuf[x_rows(k), :], LX, keep_x, keep_x_ends, tiles)
+    for r in range(8):
+        cxs[pl.ds(r, LY, stride=8), :] = tiles[r]
+
+    def spread(src, dst, n, along_x, size, least=1, most=99):
         peers, me = (x_peers, gx) if along_x else (y_peers, gy)
         mine = pl.ds(pl.multiple_of(me * size, 8), size)
-        for peer in peers:
-            pltpu.make_async_remote_copy(
-                src_ref=src.at[pl.ds(pl.multiple_of(peer * size, 8), size), :],
-                dst_ref=dst.at[mine, :],
-                send_sem=send_sem.at[n],
-                recv_sem=recv_sem.at[n],
-                device_id=(peer, gy) if along_x else (gx, peer),
-                device_id_type=MESH,
-            ).start()
-        dst[mine, :] = src[mine, :]
+        for peer, hops in peers:
+            if least <= hops <= most:
+                pltpu.make_async_remote_copy(
+                    src_ref=src.at[pl.ds(pl.multiple_of(peer * size, 8), size), :],
+                    dst_ref=dst.at[mine, :],
+                    send_sem=send_sem.at[n],
+                    recv_sem=recv_sem.at[n],
+                    device_id=(peer, gy) if along_x else (gx, peer),
+                    device_id_type=MESH,
+                ).start()
+        if least <= 1:
+            dst[mine, :] = src[mine, :]
 
     def arrived(dst, n, peers, size):
         piece = dst.at[pl.ds(0, (peers - 1) * size), :]
@@ -288,7 +319,10 @@
         piece = src.at[pl.ds(0, (peers - 1) * size), :]
         pltpu.make_async_copy(piece, piece, send_sem.at[n]).wait()
 
-    spread(cxs, cxr, 0, True, 8)
+    met(2)
+    spread(cxs, cxr, 0, True, 8, 1, 2)
+    for copy in flow_in:
+        copy.wait()
 
     def source_row(k, sums):
         here = [flat[f, cells(k), :] for f in range(NF)]
@@ -313,11 +347,9 @@
     for r in range(8):
         xs[pl.ds(r, LY, stride=8), :] = sums[r]
 
-    tiles = {}
-    keep_factor(lambda k: vbuf[y_rows(k), :], LY, keep_y, keep_y_ends, tiles)
-    for r in range(8):
-        cys[pl.ds(r, LX, stride=8), :] = tiles[r]
-    spread(cys, cyr, 1, False, 16)
+    for stage in range(3, STAGES):
+        met(stage)
+        spread(cxs, cxr, 0, True, 8, stage, stage)
 
     half = 0.5 * ADVECT
     pl.when(has_left)(y_up.wait_recv)
@@ -339,7 +371,9 @@
         for f in range(NF):
             row = pl.ds(r + f, LY, stride=8)
             xs[row, :] = xs[row, :] + speed * around[f]
+    met(STAGES)
     spread(xs, xr, 2, True, 8)
+    spread(cxs, cxr, 0, True, 8, STAGES)
 
     def x_down_row(k, before):
         result = []
@@ -362,15 +396,20 @@
     tail = lax.fori_loop(1, LX - 1, x_down_row, (slab,) * NF)
     lax.fori_loop(0, LX - 3, x_up_row, tail)
 
+    tiles = {}
+    keep_factor(lambda k: vbuf[y_rows(k), :], LY, keep_y, keep_y_ends, tiles)
+    for r in range(8):
+        cys[pl.ds(r, LX, stride=8), :] = tiles[r]
+    spread(cys, cyr, 1, False, 16)
+
     arrived(cxr, 0, PX, 8)
     interface_factor(cxr, lambda b: 8 * b, PX, xi)
+    arrived(xr, 2, PX, 8)
+    interface_solve(xr, xb, lambda b: 8 * b, PX, xi)
+    spread(xb, xg, 3, True, 8)
     arrived(cyr, 1, PY, 16)
     for t in range(2):
         interface_factor(cyr, lambda b, t=t: 16 * b + 8 * t, PY, yi[t])
-
-    arrived(xr, 2, PX, 8)
-    interface_solve(xr, xb, lambda b: 8 * b, PX, xi)
-    spread(xb, xg, 3, True, 8)
     arrived(xg, 3, PX, 8)
 
     for f in range(NF):
@@ -490,6 +529,7 @@
             pltpu.SemaphoreType.DMA((6,)),
             pltpu.SemaphoreType.DMA((4,)),
             pltpu.SemaphoreType.DMA((4,)),
+            pltpu.SemaphoreType.REGULAR((STAGES - 1,)),
         ],
         compiler_params=pltpu.CompilerParams(collective_id=0, has_side_effects=True),
     )(flow_state, viscosity.reshape(rows, NZ))

time: 36.9 us -> 40 us (1.084)
  Pallas kernels: 36.8 us -> 39.9 us
    pallas_call x1, Pallas kernels: 35.7 us -> 38.9 us  [per_device(): pl.pallas_call(kernel, out_shape=[vmem(NF, rows, NZ), vmem(2, rows, NZ),...]
where the time goes in v3:
time: 40 us; the launch traced here: 39.9 us
  Pallas kernels  39.9 us (100%)
    pallas_call x1, Pallas kernels, per_device(): pl.pallas_call(kernel, out_shape=[vmem(NF, rows, NZ), vmem(2, rows, NZ),...  38.9 us
    pallas_call x1, Pallas kernels, per_device(): pl.pallas_call(assemble, out_shape=jax.ShapeDtypeStruct((NF, rows, NZ), f...  1.04 us

profile of v3, /device:TPU:1, one launch (start us, length us, event | category | flops | bytes accessed | tf_op | source)
XLA Modules:
  0.0 39.9 jit_solution(1687399998006174244)
XLA Ops:
  0.0 38.9 %shard_map.28 = (f32[4,512,128]{2,1,0:T(8,128)S(1)}, f32[2,512,128]{2,1,0:T(8,128)S(1)}, f32[2,512,128]{2,1,0:T(8,128)S(1)}, f32[128,128]{1,0:T(8,128)S(1)}) custom-call(f32[4,16,32,128]{3,2,1,0:T(8,128)} %flow.1, f32[512,128]{1,0:T(8,128)} %bitcast.2), custom_call_target="tpu_custom_call" | custom-call | tf_op jit(solution)/shard_map/pallas_call | solution.py:502
  38.9 1.0 %shard_map.29 = f32[4,512,128]{2,1,0:T(8,128)} custom-call(f32[4,512,128]{2,1,0:T(8,128)S(1)} %get-tuple-element.9.inner, f32[2,512,128]{2,1,0:T(8,128)S(1)} %get-tuple-element.10.first, f32[2,512,128]{2,1,0:T(8,128)S(1)} %get-tuple-element.11.last, f32[128,128]{1,0:T(8,128)S(1)} %get-tuple-element.12.ends), custom_call_target="tpu_custom_call" | custom-call | tf_op jit(solution)/shard_map/pallas_call | solution.py:536

commit v4 on v2

--- a/solution.py
+++ b/solution.py
@@ -138,17 +138,17 @@
 
 def far_first(size_a, size_b):
     hops = lambda d, size: min(d, size - d)
-    offsets = [(a, b) for a in range(size_a) for b in range(size_b) if (a, b) != (0, 0)]
+    offsets = [(a, b) for a in range(size_a) for b in range(size_b)]
     return sorted(offsets, key=lambda o: -hops(o[0], size_a) - hops(o[1], size_b))
 
 
 def kernel(flow, visc, inner_y, first_y, last_y, yg, flat, vbuf, cur, inner, part, *rest):
     inv_x, low_x, rat_x, first_x, last_x = rest[0:5]
     inv_y, low_y, rat_y = rest[5:8]
-    xi, yi = rest[8:11], (rest[11:14], rest[14:17])
-    cxs, cxr, cys, cyr, xs, xr, xb, xg, ys, yr, yb = rest[17:28]
-    xh_low, xh_high, yh_low, yh_high = rest[28:32]
-    in_sem, send_sem, recv_sem, halo_send, halo_recv = rest[32:]
+    xi, yi = rest[8:11], rest[11:14]
+    cxs, cxr, cys, cyr, xs, xr, xb, xg, ys, yr, yb = rest[14:25]
+    xh_low, xh_high, yh_low, yh_high = rest[25:29]
+    in_sem, send_sem, recv_sem, halo_send, halo_recv, meet = rest[29:]
     gx, gy = lax.axis_index("gx"), lax.axis_index("gy")
 
     barrier = pltpu.get_barrier_semaphore()
@@ -156,18 +156,25 @@
     ring_x, ring_y = PX // ring_z, PY // cores
     cx, cz = lax.div(gx, ring_z), lax.rem(gx, ring_z)
     cy, cc = lax.div(gy, cores), lax.rem(gy, cores)
-    x_peers = [
-        lax.rem(cx + dx, ring_x) * ring_z + lax.rem(cz + dz, ring_z)
-        for dx, dz in far_first(ring_x, ring_z)
-    ]
-    y_peers = [
-        lax.rem(cy + dy, ring_y) * cores + lax.rem(cc + dc, cores)
-        for dy, dc in far_first(ring_y, cores)
-    ]
-    for peer in x_peers:
-        pl.semaphore_signal(barrier, inc=1, device_id=(peer, gy), device_id_type=MESH)
-    for peer in y_peers:
-        pl.semaphore_signal(barrier, inc=1, device_id=(gx, peer), device_id_type=MESH)
+    other = cy * cores + 1 - cc
+    piece = LX * 8 // ring_y
+
+    def on_x(dx, dz):
+        return lax.rem(cx + dx, ring_x) * ring_z + lax.rem(cz + dz, ring_z)
+
+    x_peers = [on_x(dx, dz) for dx, dz in far_first(ring_x, ring_z)]
+    y_peers = [lax.rem(cy + dy, ring_y) for dy, _ in far_first(ring_y, 1)]
+    column = [(on_x(dx, 0), gy) for dx, _ in far_first(ring_x, 1)[:-1]]
+    up, down = (lax.rem(gx + 1, PX), gy), (lax.rem(gx + PX - 1, PX), gy)
+    right, left = (gx, lax.rem(gy + 1, PY)), (gx, lax.rem(gy + PY - 1, PY))
+    known = [(on_x(0, dz), other) for _, dz in far_first(1, ring_z)] + column + [up, down]
+    known += [(gx, chip * cores + core) for chip in y_peers[:-1] for core in range(cores)]
+
+    def greet(sem, devices):
+        for device in devices:
+            pl.semaphore_signal(sem, inc=1, device_id=device, device_id_type=MESH)
+
+    greet(barrier, known)
 
     visc_in = pltpu.make_async_copy(visc, vbuf, in_sem.at[0])
     visc_in.start()
@@ -245,7 +252,8 @@
 
     for copy in flow_in:
         copy.wait()
-    pl.semaphore_wait(barrier, PX - 1 + PY - 1)
+    pl.semaphore_wait(barrier, len(known))
+    greet(meet, column)
 
     def halo(n, src, dst, device):
         return pltpu.make_async_remote_copy(
@@ -257,38 +265,63 @@
             device_id_type=MESH,
         )
 
-    x_up = halo(0, flat.at[:, cells(LX - 1), :], xh_low, (lax.rem(gx + 1, PX), gy))
-    x_down = halo(1, flat.at[:, cells(0), :], xh_high, (lax.rem(gx + PX - 1, PX), gy))
-    y_up = halo(2, flow.at[:, :, LY - 1, :], yh_low, (gx, lax.rem(gy + 1, PY)))
-    y_down = halo(3, flow.at[:, :, 0, :], yh_high, (gx, lax.rem(gy + PY - 1, PY)))
+    x_up = halo(0, flat.at[:, cells(LX - 1), :], xh_low, up)
+    x_down = halo(1, flat.at[:, cells(0), :], xh_high, down)
+    y_up = halo(2, flow.at[:, :, LY - 1, :], yh_low, right)
+    y_down = halo(3, flow.at[:, :, 0, :], yh_high, left)
     pl.when(has_up)(x_up.start)
     pl.when(has_down)(x_down.start)
     pl.when(has_right)(y_up.start)
     pl.when(has_left)(y_down.start)
 
-    def spread(src, dst, n, along_x, size):
-        peers, me = (x_peers, gx) if along_x else (y_peers, gy)
-        mine = pl.ds(pl.multiple_of(me * size, 8), size)
-        for peer in peers:
-            pltpu.make_async_remote_copy(
-                src_ref=src.at[pl.ds(pl.multiple_of(peer * size, 8), size), :],
-                dst_ref=dst.at[mine, :],
-                send_sem=send_sem.at[n],
-                recv_sem=recv_sem.at[n],
-                device_id=(peer, gy) if along_x else (gx, peer),
-                device_id_type=MESH,
-            ).start()
-        dst[mine, :] = src[mine, :]
-
-    def arrived(dst, n, peers, size):
-        piece = dst.at[pl.ds(0, (peers - 1) * size), :]
-        pltpu.make_async_copy(piece, piece, recv_sem.at[n]).wait()
-
-    def departed(src, n, peers, size):
-        piece = src.at[pl.ds(0, (peers - 1) * size), :]
-        pltpu.make_async_copy(piece, piece, send_sem.at[n]).wait()
-
-    spread(cxs, cxr, 0, True, 8)
+    def send(src, there, dst, here, size, n, device):
+        return pltpu.make_async_remote_copy(
+            src_ref=src.at[pl.ds(pl.multiple_of(there * size, 8), size), :],
+            dst_ref=dst.at[pl.ds(pl.multiple_of(here * size, 8), size), :],
+            send_sem=send_sem.at[n],
+            recv_sem=recv_sem.at[n],
+            device_id=device,
+            device_id_type=MESH,
+        )
+
+    def spread_x(src, dst, n):
+        for peer in x_peers:
+            send(src, peer, dst, gx, 8, n, (peer, other)).start()
+
+    def gather_y(src, dst, n):
+        for chip in y_peers[:-1]:
+            send(src, chip, dst, gy, piece, n, (gx, chip * cores + 1)).start()
+        near = send(src, cy, dst, gy, piece, n, (gx, other))
+        pl.when(cc == 0)(near.start)
+
+        @pl.when(cc == 1)
+        def _():
+            dst[pl.ds(pl.multiple_of(gy * piece, 8), piece), :] = src[
+                pl.ds(pl.multiple_of(cy * piece, 8), piece), :
+            ]
+
+    def spread_y(src, dst, n):
+        for chip in y_peers[:-1]:
+            for core in range(cores):
+                peer = chip * cores + core
+                send(src, peer, dst, cy, piece, n, (gx, peer)).start()
+        send(src, other, dst, cy, piece, n, (gx, other)).start()
+        dst[pl.ds(pl.multiple_of(cy * piece, 8), piece), :] = src[
+            pl.ds(pl.multiple_of(gy * piece, 8), piece), :
+        ]
+
+    def take(ref, sem, n, rows):
+        part = ref.at[pl.ds(0, rows), :]
+        pltpu.make_async_copy(part, part, sem.at[n]).wait()
+
+    def arrived(dst, n, rows):
+        take(dst, recv_sem, n, rows)
+
+    def departed(src, n, rows):
+        take(src, send_sem, n, rows)
+
+    all_x = 8 * PX
+    to_core_1 = (PY - 1) * piece
 
     def source_row(k, sums):
         here = [flat[f, cells(k), :] for f in range(NF)]
@@ -313,11 +346,13 @@
     for r in range(8):
         xs[pl.ds(r, LY, stride=8), :] = sums[r]
 
+    pl.semaphore_wait(meet, len(column))
+    spread_x(cxs, cxr, 0)
     tiles = {}
     keep_factor(lambda k: vbuf[y_rows(k), :], LY, keep_y, keep_y_ends, tiles)
     for r in range(8):
         cys[pl.ds(r, LX, stride=8), :] = tiles[r]
-    spread(cys, cyr, 1, False, 16)
+    gather_y(cys, cyr, 1)
 
     half = 0.5 * ADVECT
     pl.when(has_left)(y_up.wait_recv)
@@ -339,7 +374,7 @@
         for f in range(NF):
             row = pl.ds(r + f, LY, stride=8)
             xs[row, :] = xs[row, :] + speed * around[f]
-    spread(xs, xr, 2, True, 8)
+    spread_x(xs, xr, 2)
 
     def x_down_row(k, before):
         result = []
@@ -362,16 +397,20 @@
     tail = lax.fori_loop(1, LX - 1, x_down_row, (slab,) * NF)
     lax.fori_loop(0, LX - 3, x_up_row, tail)
 
-    arrived(cxr, 0, PX, 8)
+    arrived(cxr, 0, all_x)
     interface_factor(cxr, lambda b: 8 * b, PX, xi)
-    arrived(cyr, 1, PY, 16)
-    for t in range(2):
-        interface_factor(cyr, lambda b, t=t: 16 * b + 8 * t, PY, yi[t])
-
-    arrived(xr, 2, PX, 8)
+    arrived(xr, 2, all_x)
     interface_solve(xr, xb, lambda b: 8 * b, PX, xi)
-    spread(xb, xg, 3, True, 8)
-    arrived(xg, 3, PX, 8)
+    spread_x(xb, xg, 3)
+
+    @pl.when(cc == 1)
+    def _():
+        arrived(cyr, 1, to_core_1)
+        for t in range(piece // 8):
+            base = lambda b, t=t: piece * b + 8 * t
+            interface_factor(cyr, base, PY, [ref.at[t] for ref in yi])
+
+    arrived(xg, 3, all_x)
 
     for f in range(NF):
         kind = KIND_OF[f]
@@ -395,7 +434,7 @@
         for q in range(1, 8):
             total = total + part[pl.ds(64 * k + q, 8, stride=8), :]
         ys[pl.ds(8 * k, 8), :] = total
-    spread(ys, yr, 4, False, 16)
+    gather_y(ys, yr, 4)
 
     before = [edge] * NF
     for k in range(1, LY - 1):
@@ -413,22 +452,35 @@
             after[f] = inner[f, rows, :] + rat_y[KIND_OF[f], rows, :] * after[f]
             inner_y[f, y_rows(k), :] = after[f]
 
-    arrived(yr, 4, PY, 16)
-    for t in range(2):
-        interface_solve(yr, yb, lambda b, t=t: 16 * b + 8 * t, PY, yi[t])
-    spread(yb, yg, 5, False, 16)
+    @pl.when(cc == 1)
+    def _():
+        arrived(yr, 4, to_core_1)
+        for t in range(piece // 8):
+            base = lambda b, t=t: piece * b + 8 * t
+            interface_solve(yr, yb, base, PY, [ref.at[t] for ref in yi])
+        spread_y(yb, yg, 5)
 
     pl.when(has_up)(x_up.wait_send)
     pl.when(has_down)(x_down.wait_send)
     pl.when(has_right)(y_up.wait_send)
     pl.when(has_left)(y_down.wait_send)
-    departed(cxs, 0, PX, 8)
-    departed(cys, 1, PY, 16)
-    departed(xs, 2, PX, 8)
-    departed(xb, 3, PX, 8)
-    departed(ys, 4, PY, 16)
-    departed(yb, 5, PY, 16)
-    arrived(yg, 5, PY, 16)
+    departed(cxs, 0, all_x)
+    departed(xs, 2, all_x)
+    departed(xb, 3, all_x)
+
+    @pl.when(cc == 0)
+    def _():
+        departed(cys, 1, ring_y * piece)
+        departed(ys, 4, ring_y * piece)
+        arrived(yg, 5, ring_y * piece)
+
+    @pl.when(cc == 1)
+    def _():
+        if ring_y > 1:
+            departed(cys, 1, (ring_y - 1) * piece)
+            departed(ys, 4, (ring_y - 1) * piece)
+            arrived(yg, 5, (ring_y - 1) * piece)
+        departed(yb, 5, to_core_1)
 
 
 CHUNK = 4
@@ -466,7 +518,7 @@
             vmem(NF, rows, NZ),
             vmem(2, rows, NZ),
             vmem(2, rows, NZ),
-            vmem(16 * PY, NZ),
+            vmem(8 * LX, NZ),
         ],
         in_specs=[pl.BlockSpec(memory_space=pl.ANY)] * 2,
         out_specs=[in_vmem] * 4,
@@ -478,11 +530,13 @@
             vmem(LX * 64, NZ),
             *[vmem(2, rows, NZ)] * 8,
             *[vmem(PX + 1, 8, NZ)] * 3,
-            *[vmem(PY + 1, 8, NZ)] * 6,
+            *[vmem(8, PY + 1, 8, NZ)] * 3,
             *[vmem(8 * PX, NZ)] * 2,
-            *[vmem(16 * PY, NZ)] * 2,
+            vmem(8 * LX, NZ),
+            vmem(16 * LX, NZ),
             *[vmem(8 * PX, NZ)] * 4,
-            *[vmem(16 * PY, NZ)] * 3,
+            vmem(8 * LX, NZ),
+            *[vmem(16 * LX, NZ)] * 2,
             *[vmem(NF, LY, NZ)] * 2,
             *[vmem(NF, LX, NZ)] * 2,
             pltpu.SemaphoreType.DMA((1 + LX,)),
@@ -490,6 +544,7 @@
             pltpu.SemaphoreType.DMA((6,)),
             pltpu.SemaphoreType.DMA((4,)),
             pltpu.SemaphoreType.DMA((4,)),
+            pltpu.SemaphoreType.REGULAR,
         ],
         compiler_params=pltpu.CompilerParams(collective_id=0, has_side_effects=True),
     )(flow_state, viscosity.reshape(rows, NZ))

time: 36.9 us -> 35.5 us (0.962)
  Pallas kernels: 36.8 us -> 35.4 us
    pallas_call x1, Pallas kernels: 35.7 us -> 34.4 us  [per_device(): pl.pallas_call(kernel, out_shape=[vmem(NF, rows, NZ), vmem(2, rows, NZ),...]
where the time goes in v4:
time: 35.5 us; the launch traced here: 35.4 us
  Pallas kernels  35.4 us (100%)
    pallas_call x1, Pallas kernels, per_device(): pl.pallas_call(kernel, out_shape=[vmem(NF, rows, NZ), vmem(2, rows, NZ),...  34.4 us
    pallas_call x1, Pallas kernels, per_device(): pl.pallas_call(assemble, out_shape=jax.ShapeDtypeStruct((NF, rows, NZ), f...  1.04 us

profile of v4, /device:TPU:1, one launch (start us, length us, event | category | flops | bytes accessed | tf_op | source)
XLA Modules:
  0.0 35.4 jit_solution(8895867535812445596)
XLA Ops:
  0.0 34.4 %shard_map.28 = (f32[4,512,128]{2,1,0:T(8,128)S(1)}, f32[2,512,128]{2,1,0:T(8,128)S(1)}, f32[2,512,128]{2,1,0:T(8,128)S(1)}, f32[128,128]{1,0:T(8,128)S(1)}) custom-call(f32[4,16,32,128]{3,2,1,0:T(8,128)} %flow.1, f32[512,128]{1,0:T(8,128)} %bitcast.2), custom_call_target="tpu_custom_call" | custom-call | tf_op jit(solution)/shard_map/pallas_call | solution.py:515
  34.4 1.0 %shard_map.29 = f32[4,512,128]{2,1,0:T(8,128)} custom-call(f32[4,512,128]{2,1,0:T(8,128)S(1)} %get-tuple-element.9.inner, f32[2,512,128]{2,1,0:T(8,128)S(1)} %get-tuple-element.10.first, f32[2,512,128]{2,1,0:T(8,128)S(1)} %get-tuple-element.11.last, f32[128,128]{1,0:T(8,128)S(1)} %get-tuple-element.12.ends), custom_call_target="tpu_custom_call" | custom-call | tf_op jit(solution)/shard_map/pallas_call | solution.py:551

commit v5 on v4

--- a/solution.py
+++ b/solution.py
@@ -265,21 +265,33 @@
             device_id_type=MESH,
         )
 
-    x_up = halo(0, flat.at[:, cells(LX - 1), :], xh_low, up)
-    x_down = halo(1, flat.at[:, cells(0), :], xh_high, down)
-    y_up = halo(2, flow.at[:, :, LY - 1, :], yh_low, right)
-    y_down = halo(3, flow.at[:, :, 0, :], yh_high, left)
-    pl.when(has_up)(x_up.start)
-    pl.when(has_down)(x_down.start)
+    strip = LY // ring_x
+    row_order = [dx for dx, _ in far_first(ring_x, 1)]
+
+    def strip_at(n, device_x):
+        return pl.multiple_of(lax.rem(device_x + row_order[n], ring_x) * strip, 8)
+
+    def x_halo(n, toward, k, dst):
+        at = strip_at(n % ring_x, lax.div(toward[0], ring_z))
+        src = flat.at[:, pl.ds((k + 1) * wide + Y0 + at, strip), :]
+        return halo(n, src, dst.at[:, pl.ds(at, strip), :], toward)
+
+    x_up = [x_halo(n, up, LX - 1, xh_low) for n in range(ring_x)]
+    x_down = [x_halo(ring_x + n, down, 0, xh_high) for n in range(ring_x)]
+    y_up = halo(2 * ring_x, flow.at[:, :, LY - 1, :], yh_low, right)
+    y_down = halo(2 * ring_x + 1, flow.at[:, :, 0, :], yh_high, left)
     pl.when(has_right)(y_up.start)
     pl.when(has_left)(y_down.start)
-
-    def send(src, there, dst, here, size, n, device):
+    for n in range(ring_x):
+        pl.when(has_up)(x_up[n].start)
+        pl.when(has_down)(x_down[n].start)
+
+    def send(src, there, dst, here, size, n, device, arrival=None):
         return pltpu.make_async_remote_copy(
             src_ref=src.at[pl.ds(pl.multiple_of(there * size, 8), size), :],
             dst_ref=dst.at[pl.ds(pl.multiple_of(here * size, 8), size), :],
             send_sem=send_sem.at[n],
-            recv_sem=recv_sem.at[n],
+            recv_sem=recv_sem.at[n if arrival is None else arrival],
             device_id=device,
             device_id_type=MESH,
         )
@@ -348,11 +360,6 @@
 
     pl.semaphore_wait(meet, len(column))
     spread_x(cxs, cxr, 0)
-    tiles = {}
-    keep_factor(lambda k: vbuf[y_rows(k), :], LY, keep_y, keep_y_ends, tiles)
-    for r in range(8):
-        cys[pl.ds(r, LX, stride=8), :] = tiles[r]
-    gather_y(cys, cyr, 1)
 
     half = 0.5 * ADVECT
     pl.when(has_left)(y_up.wait_recv)
@@ -367,14 +374,18 @@
                 row = pl.ds(at * 8 + r, 1)
                 total = jnp.sum(weight[kind, y_rows(at), :] * change, axis=0, keepdims=True)
                 xs[row, :] = xs[row, :] + total
-    pl.when(has_down)(x_up.wait_recv)
-    pl.when(has_up)(x_down.wait_recv)
-    for r, at, around, sign in ((0, 0, xh_low, half), (NF, LX - 1, xh_high, -half)):
-        speed = sign * flat[0, cells(at), :]
-        for f in range(NF):
-            row = pl.ds(r + f, LY, stride=8)
-            xs[row, :] = xs[row, :] + speed * around[f]
-    spread_x(xs, xr, 2)
+    for n in range(ring_x):
+        at = strip_at(n, cx)
+        pl.when(has_down)(x_up[n].wait_recv)
+        pl.when(has_up)(x_down[n].wait_recv)
+        for r, edge_k, around, sign in ((0, 0, xh_low, half), (NF, LX - 1, xh_high, -half)):
+            speed = sign * flat[0, pl.ds((edge_k + 1) * wide + Y0 + at, strip), :]
+            for f in range(NF):
+                row = pl.ds(8 * at + r + f, strip, stride=8)
+                xs[row, :] = xs[row, :] + speed * around[f, pl.ds(at, strip), :]
+        for _, dz in far_first(1, ring_z):
+            peer = on_x(row_order[n], dz)
+            send(xs, peer, xr, gx, 8, 2, (peer, other)).start()
 
     def x_down_row(k, before):
         result = []
@@ -397,11 +408,19 @@
     tail = lax.fori_loop(1, LX - 1, x_down_row, (slab,) * NF)
     lax.fori_loop(0, LX - 3, x_up_row, tail)
 
+    tiles = {}
+    keep_factor(lambda k: vbuf[y_rows(k), :], LY, keep_y, keep_y_ends, tiles)
+    for r in range(8):
+        cys[pl.ds(r, LX, stride=8), :] = tiles[r]
+    gather_y(cys, cyr, 1)
+
     arrived(cxr, 0, all_x)
     interface_factor(cxr, lambda b: 8 * b, PX, xi)
     arrived(xr, 2, all_x)
     interface_solve(xr, xb, lambda b: 8 * b, PX, xi)
-    spread_x(xb, xg, 3)
+    for dx, dz in far_first(ring_x, ring_z):
+        peer = on_x(dx, dz)
+        send(xb, peer, xg, gx, 8, 3, (peer, other), 6 + (ring_x - dx) % ring_x).start()
 
     @pl.when(cc == 1)
     def _():
@@ -410,22 +429,28 @@
             base = lambda b, t=t: piece * b + 8 * t
             interface_factor(cyr, base, PY, [ref.at[t] for ref in yi])
 
-    arrived(xg, 3, all_x)
-
-    for f in range(NF):
-        kind = KIND_OF[f]
-        start, end = xg[pl.ds(f, LY, stride=8), :], xg[pl.ds(NF + f, LY, stride=8), :]
-
-        def x_row(k, carry, f=f, kind=kind, start=start, end=end):
-            rows = x_rows(k)
-            value = inner[f, rows, :] + first_x[kind, rows, :] * start + last_x[kind, rows, :] * end
-            cur[f, rows, :] = value
-            for r, weight in ((f, first_y), (NF + f, last_y)):
-                share = weight[kind, rows, :] * value
-                total = share[0:8]
-                for q in range(8, LY, 8):
-                    total = total + share[q : q + 8]
-                part[pl.ds(pl.multiple_of(k * 64, 8) + 8 * r, 8), :] = total
+    for n in range(ring_x):
+        dx = row_order[ring_x - 1 - n]
+        at = pl.multiple_of(lax.rem(cx + dx, ring_x) * strip, 8)
+        arrived(xg, 6 + dx, 8 * strip)
+        starts = [xg[pl.ds(8 * at + f, strip, stride=8), :] for f in range(NF)]
+        ends = [xg[pl.ds(8 * at + NF + f, strip, stride=8), :] for f in range(NF)]
+
+        def x_row(k, carry, n=n, at=at, starts=starts, ends=ends):
+            rows = pl.ds(pl.multiple_of(k * LY + at, 8), strip)
+            shares = pl.multiple_of(k * 64, 8)
+            for f in range(NF):
+                kind = KIND_OF[f]
+                value = (
+                    inner[f, rows, :]
+                    + first_x[kind, rows, :] * starts[f]
+                    + last_x[kind, rows, :] * ends[f]
+                )
+                cur[f, rows, :] = value
+                for r, weight in ((f, first_y), (NF + f, last_y)):
+                    share = weight[kind, rows, :] * value
+                    here = pl.ds(shares + 8 * r, 8)
+                    part[here, :] = share if n == 0 else part[here, :] + share
             return carry
 
         lax.fori_loop(0, LX, x_row, 0, unroll=4)
@@ -460,8 +485,9 @@
             interface_solve(yr, yb, base, PY, [ref.at[t] for ref in yi])
         spread_y(yb, yg, 5)
 
-    pl.when(has_up)(x_up.wait_send)
-    pl.when(has_down)(x_down.wait_send)
+    for n in range(ring_x):
+        pl.when(has_up)(x_up[n].wait_send)
+        pl.when(has_down)(x_down[n].wait_send)
     pl.when(has_right)(y_up.wait_send)
     pl.when(has_left)(y_down.wait_send)
     departed(cxs, 0, all_x)
@@ -541,9 +567,9 @@
             *[vmem(NF, LX, NZ)] * 2,
             pltpu.SemaphoreType.DMA((1 + LX,)),
             pltpu.SemaphoreType.DMA((6,)),
-            pltpu.SemaphoreType.DMA((6,)),
-            pltpu.SemaphoreType.DMA((4,)),
-            pltpu.SemaphoreType.DMA((4,)),
+            pltpu.SemaphoreType.DMA((10,)),
+            pltpu.SemaphoreType.DMA((10,)),
+            pltpu.SemaphoreType.DMA((10,)),
             pltpu.SemaphoreType.REGULAR,
         ],
         compiler_params=pltpu.CompilerParams(collective_id=0, has_side_effects=True),

time: 35.5 us -> 36 us (1.014)
  Pallas kernels: 35.4 us -> 35.9 us
    pallas_call x1, Pallas kernels: 34.4 us -> 34.8 us  [per_device(): pl.pallas_call(kernel, out_shape=[vmem(NF, rows, NZ), vmem(2, rows, NZ),...]
where the time goes in v5:
time: 36 us; the launch traced here: 35.9 us
  Pallas kernels  35.9 us (100%)
    pallas_call x1, Pallas kernels, per_device(): pl.pallas_call(kernel, out_shape=[vmem(NF, rows, NZ), vmem(2, rows, NZ),...  34.8 us
    pallas_call x1, Pallas kernels, per_device(): pl.pallas_call(assemble, out_shape=jax.ShapeDtypeStruct((NF, rows, NZ), f...  1.04 us

profile of v5, /device:TPU:1, one launch (start us, length us, event | category | flops | bytes accessed | tf_op | source)
XLA Modules:
  0.0 35.9 jit_solution(12864802589844727555)
XLA Ops:
  0.0 34.8 %shard_map.28 = (f32[4,512,128]{2,1,0:T(8,128)S(1)}, f32[2,512,128]{2,1,0:T(8,128)S(1)}, f32[2,512,128]{2,1,0:T(8,128)S(1)}, f32[128,128]{1,0:T(8,128)S(1)}) custom-call(f32[4,16,32,128]{3,2,1,0:T(8,128)} %flow.1, f32[512,128]{1,0:T(8,128)} %bitcast.2), custom_call_target="tpu_custom_call" | custom-call | tf_op jit(solution)/shard_map/pallas_call | solution.py:541
  34.8 1.0 %shard_map.29 = f32[4,512,128]{2,1,0:T(8,128)} custom-call(f32[4,512,128]{2,1,0:T(8,128)S(1)} %get-tuple-element.9.inner, f32[2,512,128]{2,1,0:T(8,128)S(1)} %get-tuple-element.10.first, f32[2,512,128]{2,1,0:T(8,128)S(1)} %get-tuple-element.11.last, f32[128,128]{1,0:T(8,128)S(1)} %get-tuple-element.12.ends), custom_call_target="tpu_custom_call" | custom-call | tf_op jit(solution)/shard_map/pallas_call | solution.py:577

commit v6 on v4

--- a/solution.py
+++ b/solution.py
@@ -288,6 +288,12 @@
         for peer in x_peers:
             send(src, peer, dst, gx, 8, n, (peer, other)).start()
 
+    def spread_part(src, dst, n, own_row):
+        for dx, dz in far_first(ring_x, ring_z):
+            if (dx == 0) == own_row:
+                peer = on_x(dx, dz)
+                send(src, peer, dst, gx, 8, n, (peer, other)).start()
+
     def gather_y(src, dst, n):
         for chip in y_peers[:-1]:
             send(src, chip, dst, gy, piece, n, (gx, chip * cores + 1)).start()
@@ -320,6 +326,7 @@
     def departed(src, n, rows):
         take(src, send_sem, n, rows)
 
+    spread_part(cxs, cxr, 0, True)
     all_x = 8 * PX
     to_core_1 = (PY - 1) * piece
 
@@ -347,7 +354,7 @@
         xs[pl.ds(r, LY, stride=8), :] = sums[r]
 
     pl.semaphore_wait(meet, len(column))
-    spread_x(cxs, cxr, 0)
+    spread_part(cxs, cxr, 0, False)
     tiles = {}
     keep_factor(lambda k: vbuf[y_rows(k), :], LY, keep_y, keep_y_ends, tiles)
     for r in range(8):

time: 35.5 us -> 35.2 us (level)
  no operation moved by 1% of the time
where the time goes in v6:
time: 35.2 us; the launch traced here: 35.1 us
  Pallas kernels  35.1 us (100%)
    pallas_call x1, Pallas kernels, per_device(): pl.pallas_call(kernel, out_shape=[vmem(NF, rows, NZ), vmem(2, rows, NZ),...  34 us
    pallas_call x1, Pallas kernels, per_device(): pl.pallas_call(assemble, out_shape=jax.ShapeDtypeStruct((NF, rows, NZ), f...  1.04 us

profile of v6, /device:TPU:1, one launch (start us, length us, event | category | flops | bytes accessed | tf_op | source)
XLA Modules:
  0.0 35.1 jit_solution(9168984789897226277)
XLA Ops:
  0.0 34.0 %shard_map.28 = (f32[4,512,128]{2,1,0:T(8,128)S(1)}, f32[2,512,128]{2,1,0:T(8,128)S(1)}, f32[2,512,128]{2,1,0:T(8,128)S(1)}, f32[128,128]{1,0:T(8,128)S(1)}) custom-call(f32[4,16,32,128]{3,2,1,0:T(8,128)} %flow.1, f32[512,128]{1,0:T(8,128)} %bitcast.2), custom_call_target="tpu_custom_call" | custom-call | tf_op jit(solution)/shard_map/pallas_call | solution.py:522
  34.1 1.0 %shard_map.29 = f32[4,512,128]{2,1,0:T(8,128)} custom-call(f32[4,512,128]{2,1,0:T(8,128)S(1)} %get-tuple-element.9.inner, f32[2,512,128]{2,1,0:T(8,128)S(1)} %get-tuple-element.10.first, f32[2,512,128]{2,1,0:T(8,128)S(1)} %get-tuple-element.11.last, f32[128,128]{1,0:T(8,128)S(1)} %get-tuple-element.12.ends), custom_call_target="tpu_custom_call" | custom-call | tf_op jit(solution)/shard_map/pallas_call | solution.py:558

commit v7 on v6

--- a/solution.py
+++ b/solution.py
@@ -164,6 +164,7 @@
 
     x_peers = [on_x(dx, dz) for dx, dz in far_first(ring_x, ring_z)]
     y_peers = [lax.rem(cy + dy, ring_y) for dy, _ in far_first(ring_y, 1)]
+    col_dx = [dx for dx, _ in far_first(ring_x, 1)[:-1]]
     column = [(on_x(dx, 0), gy) for dx, _ in far_first(ring_x, 1)[:-1]]
     up, down = (lax.rem(gx + 1, PX), gy), (lax.rem(gx + PX - 1, PX), gy)
     right, left = (gx, lax.rem(gy + 1, PY)), (gx, lax.rem(gy + PY - 1, PY))
@@ -253,7 +254,8 @@
     for copy in flow_in:
         copy.wait()
     pl.semaphore_wait(barrier, len(known))
-    greet(meet, column)
+    for n, device in enumerate(column):
+        pl.semaphore_signal(meet.at[n], inc=1, device_id=device, device_id_type=MESH)
 
     def halo(n, src, dst, device):
         return pltpu.make_async_remote_copy(
@@ -353,14 +355,13 @@
     for r in range(8):
         xs[pl.ds(r, LY, stride=8), :] = sums[r]
 
-    pl.semaphore_wait(meet, len(column))
-    spread_part(cxs, cxr, 0, False)
-    tiles = {}
-    keep_factor(lambda k: vbuf[y_rows(k), :], LY, keep_y, keep_y_ends, tiles)
-    for r in range(8):
-        cys[pl.ds(r, LX, stride=8), :] = tiles[r]
-    gather_y(cys, cyr, 1)
-
+    for n in range(1, len(column) + 1):
+        came = len(column) - n
+        dx = (ring_x - col_dx[came]) % ring_x
+        pl.semaphore_wait(meet.at[came], 1)
+        for _, dz in far_first(1, ring_z):
+            peer = on_x(dx, dz)
+            send(cxs, peer, cxr, gx, 8, 0, (peer, other)).start()
     half = 0.5 * ADVECT
     pl.when(has_left)(y_up.wait_recv)
     pl.when(has_right)(y_down.wait_recv)
@@ -403,6 +404,12 @@
 
     tail = lax.fori_loop(1, LX - 1, x_down_row, (slab,) * NF)
     lax.fori_loop(0, LX - 3, x_up_row, tail)
+
+    tiles = {}
+    keep_factor(lambda k: vbuf[y_rows(k), :], LY, keep_y, keep_y_ends, tiles)
+    for r in range(8):
+        cys[pl.ds(r, LX, stride=8), :] = tiles[r]
+    gather_y(cys, cyr, 1)
 
     arrived(cxr, 0, all_x)
     interface_factor(cxr, lambda b: 8 * b, PX, xi)
@@ -551,7 +558,7 @@
             pltpu.SemaphoreType.DMA((6,)),
             pltpu.SemaphoreType.DMA((4,)),
             pltpu.SemaphoreType.DMA((4,)),
-            pltpu.SemaphoreType.REGULAR,
+            pltpu.SemaphoreType.REGULAR((3,)),
         ],
         compiler_params=pltpu.CompilerParams(collective_id=0, has_side_effects=True),
     )(flow_state, viscosity.reshape(rows, NZ))

time: 35.2 us -> 35 us (level)
  no operation moved by 1% of the time
where the time goes in v7:
time: 35 us; the launch traced here: 34.9 us
  Pallas kernels  34.9 us (100%)
    pallas_call x1, Pallas kernels, per_device(): pl.pallas_call(kernel, out_shape=[vmem(NF, rows, NZ), vmem(2, rows, NZ),...  33.9 us
    pallas_call x1, Pallas kernels, per_device(): pl.pallas_call(assemble, out_shape=jax.ShapeDtypeStruct((NF, rows, NZ), f...  1.04 us

profile of v7, /device:TPU:1, one launch (start us, length us, event | category | flops | bytes accessed | tf_op | source)
XLA Modules:
  0.0 34.9 jit_solution(6423088481825829790)
XLA Ops:
  0.0 33.9 %shard_map.28 = (f32[4,512,128]{2,1,0:T(8,128)S(1)}, f32[2,512,128]{2,1,0:T(8,128)S(1)}, f32[2,512,128]{2,1,0:T(8,128)S(1)}, f32[128,128]{1,0:T(8,128)S(1)}) custom-call(f32[4,16,32,128]{3,2,1,0:T(8,128)} %flow.1, f32[512,128]{1,0:T(8,128)} %bitcast.2), custom_call_target="tpu_custom_call" | custom-call | tf_op jit(solution)/shard_map/pallas_call | solution.py:529
  33.9 1.0 %shard_map.29 = f32[4,512,128]{2,1,0:T(8,128)} custom-call(f32[4,512,128]{2,1,0:T(8,128)S(1)} %get-tuple-element.9.inner, f32[2,512,128]{2,1,0:T(8,128)S(1)} %get-tuple-element.10.first, f32[2,512,128]{2,1,0:T(8,128)S(1)} %get-tuple-element.11.last, f32[128,128]{1,0:T(8,128)S(1)} %get-tuple-element.12.ends), custom_call_target="tpu_custom_call" | custom-call | tf_op jit(solution)/shard_map/pallas_call | solution.py:565
